TPU v7x, 32 devices: a whole 2x2x4 slice. The times are simulated.
32 devices in a mesh: section: 2 (over core), dp: 4 (over y, x), tensor: 4 (over z).
Axes of the slice: x: 2, y: 2, z: 4, core: 2. Of those that a mesh axis runs over, the one named last changes fastest.
Arguments:
- section_input: bfloat16 [2, 512, 4096], P('section', 'dp'), may hold values from -60 to 60
- weights: bfloat16 [2, 4096, 4096], P('section', 'tensor', 'dp'), may hold values from -0.1875 to 0.1875
- gains: float32 [2, 4096], P('section'), may hold values from 0.1 to 1.9
- proj_seeds: int32 [2, 2], P('section'), may hold values from 0 to 99999
- out_grad: bfloat16 [512, 4096], P('dp'), may hold values from -0.75 to 0.75
- query_grads: bfloat16 [2, 256, 4096], P('section', 'dp', 'tensor'), may hold values from -0.017944336 to 0.017944336
Outputs:
- projected_grads: float32 [2, 2, 4096], P('section', None, 'tensor')
- scores: float32 [2, 256], P(None, 'dp')
All inputs are finite; a program needn't handle non-finite values.
Results may differ from a plain program's by a relative error of at most 0.033.
Values may be sent and summed in bfloat16 or wider, within the bound.
A program may use at most 64 MiB of HBM per device.

v0:
```python
import math

import jax
import jax.numpy as jnp
from jax import lax
from jax.sharding import PartitionSpec as P

R = 64
SEQS = 2
MICRO = 16


eps = 1e-05


def passed_along(value, axis, steps):
    count = lax.axis_size(axis)
    first, last = (max(0, -steps), min(count, count - steps))
    return lax.ppermute(value, axis, [(source, source + steps) for source in range(first, last)])


def sign_table(seed_value, row_count):
    row_index = lax.broadcasted_iota(jnp.int32, (row_count, R), 0)
    col_index = lax.broadcasted_iota(jnp.int32, (row_count, R), 1)
    mixing = row_index * 40503 + col_index * 9973 + seed_value * 7919 + 12345
    mixing = mixing ^ mixing >> 13
    mixing = mixing * 1274126177
    mixing = mixing ^ mixing >> 16
    parity = mixing >> 10 & 1
    return (jnp.where(parity == 1, 1.0, -1.0) * (1.0 / math.sqrt(row_count))).astype(jnp.bfloat16)


def take_rows(table, row_start):
    return lax.dynamic_slice_in_dim(table, row_start, MICRO, 0)


def body(section_input, weights, gains, proj_seeds, out_grad, query_grads):
    section_count = lax.axis_size("section")
    section_index = lax.axis_index("section")
    data_count = lax.axis_size("dp")
    data_index = lax.axis_index("dp")
    split_count = lax.axis_size("tensor")
    split_index = lax.axis_index("tensor")
    tok_rows = section_input.shape[1]
    feature_width = section_input.shape[2]
    slice_width = feature_width // split_count
    blocks = tok_rows // MICRO
    turn_count = section_count + blocks - 1
    own_start = split_index * slice_width
    gain_row = gains[0]
    hidden_in = section_input[0].astype(jnp.float32)
    radius = jnp.sqrt(jnp.mean(hidden_in * hidden_in, axis=1, keepdims=True) + eps)
    normed = hidden_in / radius
    lifted = (normed * gain_row).astype(jnp.bfloat16)
    weight_rows = lax.all_gather(weights[0], "dp", axis=1, tiled=True)
    lifted_own = lax.dynamic_slice_in_dim(lifted, own_start, slice_width, 1)
    partial_value = jnp.dot(lifted_own, weight_rows, preferred_element_type=jnp.float32)
    summed = lax.psum(partial_value.astype(jnp.bfloat16), "tensor").astype(jnp.float32)
    sigmoid_z = jax.nn.sigmoid(summed)
    slopes = sigmoid_z * (1.0 + summed * (1.0 - sigmoid_z))
    proj_in = sign_table(proj_seeds[0, 0], feature_width)
    proj_out = sign_table(proj_seeds[0, 1], feature_width)
    in_features = jnp.dot(lifted, proj_in, preferred_element_type=jnp.float32).astype(jnp.bfloat16)
    chain_depth = section_count - 1 - section_index
    at_top = section_index == section_count - 1

    def block_grad(operands):
        upstream, slope_rows, feature_rows, grad_sum = operands
        grad_pre = (upstream.astype(jnp.float32) * slope_rows).astype(jnp.bfloat16)
        out_features = jnp.dot(grad_pre, proj_out, preferred_element_type=jnp.float32).astype(
            jnp.bfloat16
        )
        grad_sum = grad_sum + lax.dot_general(
            feature_rows, out_features, (((0,), (0,)), ((), ())), preferred_element_type=jnp.float32
        )
        own_grads = lax.dot_general(
            grad_pre, weight_rows, (((1,), (1,)), ((), ())), preferred_element_type=jnp.float32
        ).astype(jnp.bfloat16)
        return (own_grads, grad_sum)

    def block_skip(operands):
        return (jnp.zeros((MICRO, slice_width), jnp.bfloat16), operands[3])

    def prepare(turn_index, upstream_in):
        block_index = turn_index.astype(jnp.int32) - chain_depth
        active = jnp.logical_and(block_index >= 0, block_index < blocks)
        row_start = jnp.clip(block_index, 0, blocks - 1) * MICRO
        top_rows = take_rows(out_grad, row_start)
        upstream = jnp.where(at_top, top_rows, upstream_in)
        return (active, row_start, upstream)

    def turn(turn_index, loop_state):
        incoming, grad_sum = loop_state
        active, row_start, upstream = prepare(turn_index, incoming)
        own_grads, grad_sum = lax.cond(
            active,
            block_grad,
            block_skip,
            (upstream, take_rows(slopes, row_start), take_rows(in_features, row_start), grad_sum),
        )
        full_grads = lax.all_gather(own_grads, "tensor", axis=1, tiled=True)

        def finish(operands):
            upstream_rows, grad_rows, normed_rows, radius_rows = operands
            scaled = grad_rows.astype(jnp.float32) * gain_row
            mean_dot = jnp.mean(scaled * normed_rows, axis=1, keepdims=True)
            return (
                upstream_rows.astype(jnp.float32) + (scaled - normed_rows * mean_dot) / radius_rows
            ).astype(jnp.bfloat16)

        def vacant(operands):
            return jnp.zeros((MICRO, feature_width), jnp.bfloat16)

        outgoing = lax.cond(
            active,
            finish,
            vacant,
            (upstream, full_grads, take_rows(normed, row_start), take_rows(radius, row_start)),
        )
        received = passed_along(outgoing, "section", -1)
        return (received, grad_sum)

    start_state = (jnp.zeros((MICRO, feature_width), jnp.bfloat16), jnp.zeros((R, R), jnp.float32))
    received, grad_sum = lax.fori_loop(0, turn_count, turn, start_state)
    flattened = grad_sum.reshape(R * R)
    piece_width = R * R // split_count
    own_part = lax.dynamic_slice_in_dim(flattened, split_index * piece_width, piece_width, 0)
    seq_index = data_index // (data_count // SEQS)
    seq_mask = (lax.broadcasted_iota(jnp.int32, (SEQS, 1), 0) == seq_index).astype(jnp.float32)
    per_seq = seq_mask * own_part[None, :]
    grads_all = lax.psum(per_seq, "dp")
    queries = query_grads[0].astype(jnp.float32)
    partial_scores = jnp.dot(grads_all, queries.T, precision=lax.Precision.HIGHEST)
    scores = lax.psum(partial_scores, ("section", "tensor"))
    return (grads_all[None], scores)


def solution(mesh):
    in_specs = (
        P("section", "dp", None),
        P("section", "tensor", "dp"),
        P("section", None),
        P("section", None),
        P("dp", None),
        P("section", "dp", "tensor"),
    )
    out_specs = (P("section", None, "tensor"), P(None, "dp"))
    return jax.shard_map(body, mesh=mesh, in_specs=in_specs, out_specs=out_specs, check_vma=False)
```

profile of v0, /device:TPU:0, one launch (start us, length us, event | category | flops | bytes accessed | tf_op | source)
XLA Modules:
  0.0 456.5 jit_solution(3057841927889815034)
XLA Ops:
  11.0 89.1 %all-gather.3.cloned.1.call-done = bf16[1,1024,4096]{2,1,0:T(8,128)(2,1)} async-done(((bf16[1,1024,1024]{2,1,0:T(8,128)(2,1)}), bf16[1,1024,4096]{2,1,0:T(8,128)(2,1)}) %all-gather.3.cloned.1.call-update) | async-done | bytes 8388624 | tf_op jit(solution)/shard_map/all_gather | solution.py:55
  100.1 5.7 %convolution_convert_fusion.2 = bf16[128,4096]{1,0:T(8,128)(2,1)} fusion(bf16[128,4096]{1,0:T(8,128)(2,1)S(1)} %get-tuple-element.421, s32[]{:T(128)S(6)} %select_n.44, bf16[1,1024,4096]{2,1,0:T(8,128)(2,1)} %all-gather.3.cloned.1.call-done), kind=kOutput, calls=%fused_computation.21 | convolution fusion | flops 1074266112 | bytes 9699332 | tf_op jit(solution)/shard_map/dot_general | solution.py:57
  108.9 2.1 convolution_convert_fusion.3
  112.3 45.6 %all-reduce.2.cloned.1.call-done = bf16[128,4096]{1,0:T(8,128)(2,1)} async-done(((bf16[128,4096]{1,0:T(8,128)(2,1)}), bf16[128,4096]{1,0:T(8,128)(2,1)}) %all-reduce.2.cloned.1.call-update) | async-done | bytes 1048592 | tf_op jit(solution)/shard_map/psum | solution.py:58
  157.8 1.9 fusion.13
  160.4 263.4 %while.19 = (s32[]{:T(128)}, bf16[16,4096]{1,0:T(8,128)(2,1)S(1)}, f32[64,64]{1,0:T(8,128)}, s32[]{:T(128)}, pred[]{:T(512)}, /*index=5*/bf16[128,4096]{1,0:T(8,...) while((s32[]{:T(128)}, bf16[16,4096]{1,0:T(8,128)(2,1)S(1)}, ...), condition=%wide.region_8.9_spmd.clone, body=%wide.region_2.8_spmd.clone.sunk | while | flops 147674128 | bytes 13017286 | solution.py:124
  160.4 2.3 multiply_convert_fusion.9
  163.8 13.3 %all_gather.13 = bf16[16,4096]{1,0:T(8,128)(2,1)S(1)} all-gather(bf16[16,1024]{1,0:T(8,128)(2,1)S(1)} %get-tuple-element.519), channel_id=1, replica_groups=mesh['section'=2,'dp'=4,'tensor'=4] {'tensor'}, dimensions={1}, use_global_device_ids=true | all-gather | bytes 163840 | tf_op jit(solution)/shard_map/while/body/eval_jaxpr/all_gather | solution.py:101
  178.4 7.6 %collective-permute-done = bf16[16,4096]{1,0:T(8,128)(2,1)S(1)} collective-permute-done((bf16[16,4096]{1,0:T(8,128)(2,1)S(1)}, bf16[16,4096]{1,0:T(8,128)(2,1)S(1)}, u32[]{:S(2)}, u32[]{:S(2)}) %collective-permute-start) | collective-permute-done | bytes 131104 | tf_op jit(solution)/shard_map/while/body/eval_jaxpr/ppermute | solution.py:19
  186.0 2.3 multiply_convert_fusion.9
  189.3 7.4 %conditional.6 = (bf16[16,1024]{1,0:T(8,128)(2,1)S(1)}, f32[64,64]{1,0:T(8,128)}) conditional(s32[]{:T(128)} %convert_element_type.134, f32[64,64]{1,0:T(8,128)} %get-tuple-element.548, (bf16[16,4096]{1,0:T(8,128)(2,1)S(1)}, f32[128,4096]{1,0:T(8,128)S(1)}, s32[]{:T(128)}, bf16[1024,4096]{1,0:T(8,128)(2,1)}, bf16[128,64]{1,0:T(8,128)(2,1)}, ...), branch_computations={%region_3.3_spmd, %region_4.4_spmd} | conditional | flops 143152128 | bytes 10310676 | solution.py:95
  189.4 5.6 %convolution_convert_fusion = bf16[16,1024]{1,0:T(8,128)(2,1)S(1)} fusion(bf16[1024,4096]{1,0:T(8,128)(2,1)} %get-tuple-element.308, f32[128,4096]{1,0:T(8,128)S(1)} %get-tuple-element.306, s32[]{:T(128)} %get-tuple-element.307, bf16[16,4096]{1,0:T(8,128)(2,1)S(1)} %get-tuple-element.305), kind=kOutput, calls=%fused_computation.1 | convolution fusion | flops 134430720 | bytes 8814596 | tf_op jit(solution)/shard_map/while/body/eval_jaxpr/cond/branch_1_fun/dot_general | solution.py:76
  195.0 1.8 convolution_add_fusion
  196.8 13.4 %all_gather.13 = bf16[16,4096]{1,0:T(8,128)(2,1)S(1)} all-gather(bf16[16,1024]{1,0:T(8,128)(2,1)S(1)} %get-tuple-element.519), channel_id=1, replica_groups=mesh['section'=2,'dp'=4,'tensor'=4] {'tensor'}, dimensions={1}, use_global_device_ids=true | all-gather | bytes 163840 | tf_op jit(solution)/shard_map/while/body/eval_jaxpr/all_gather | solution.py:101
  210.2 2.4 conditional.7
  213.9 1.9 collective-permute-done
  215.8 2.3 multiply_convert_fusion.9
  219.1 7.4 %conditional.6 = (bf16[16,1024]{1,0:T(8,128)(2,1)S(1)}, f32[64,64]{1,0:T(8,128)}) conditional(s32[]{:T(128)} %convert_element_type.134, f32[64,64]{1,0:T(8,128)} %get-tuple-element.548, (bf16[16,4096]{1,0:T(8,128)(2,1)S(1)}, f32[128,4096]{1,0:T(8,128)S(1)}, s32[]{:T(128)}, bf16[1024,4096]{1,0:T(8,128)(2,1)}, bf16[128,64]{1,0:T(8,128)(2,1)}, ...), branch_computations={%region_3.3_spmd, %region_4.4_spmd} | conditional | flops 143152128 | bytes 10310676 | solution.py:95
  219.1 5.6 %convolution_convert_fusion = bf16[16,1024]{1,0:T(8,128)(2,1)S(1)} fusion(bf16[1024,4096]{1,0:T(8,128)(2,1)} %get-tuple-element.308, f32[128,4096]{1,0:T(8,128)S(1)} %get-tuple-element.306, s32[]{:T(128)} %get-tuple-element.307, bf16[16,4096]{1,0:T(8,128)(2,1)S(1)} %get-tuple-element.305), kind=kOutput, calls=%fused_computation.1 | convolution fusion | flops 134430720 | bytes 8814596 | tf_op jit(solution)/shard_map/while/body/eval_jaxpr/cond/branch_1_fun/dot_general | solution.py:76
  224.8 1.8 convolution_add_fusion
  226.6 13.4 %all_gather.13 = bf16[16,4096]{1,0:T(8,128)(2,1)S(1)} all-gather(bf16[16,1024]{1,0:T(8,128)(2,1)S(1)} %get-tuple-element.519), channel_id=1, replica_groups=mesh['section'=2,'dp'=4,'tensor'=4] {'tensor'}, dimensions={1}, use_global_device_ids=true | all-gather | bytes 163840 | tf_op jit(solution)/shard_map/while/body/eval_jaxpr/all_gather | solution.py:101
  240.0 2.4 conditional.7
  243.6 1.9 collective-permute-done
  245.6 2.3 multiply_convert_fusion.9
  248.9 7.4 %conditional.6 = (bf16[16,1024]{1,0:T(8,128)(2,1)S(1)}, f32[64,64]{1,0:T(8,128)}) conditional(s32[]{:T(128)} %convert_element_type.134, f32[64,64]{1,0:T(8,128)} %get-tuple-element.548, (bf16[16,4096]{1,0:T(8,128)(2,1)S(1)}, f32[128,4096]{1,0:T(8,128)S(1)}, s32[]{:T(128)}, bf16[1024,4096]{1,0:T(8,128)(2,1)}, bf16[128,64]{1,0:T(8,128)(2,1)}, ...), branch_computations={%region_3.3_spmd, %region_4.4_spmd} | conditional | flops 143152128 | bytes 10310676 | solution.py:95
  248.9 5.6 %convolution_convert_fusion = bf16[16,1024]{1,0:T(8,128)(2,1)S(1)} fusion(bf16[1024,4096]{1,0:T(8,128)(2,1)} %get-tuple-element.308, f32[128,4096]{1,0:T(8,128)S(1)} %get-tuple-element.306, s32[]{:T(128)} %get-tuple-element.307, bf16[16,4096]{1,0:T(8,128)(2,1)S(1)} %get-tuple-element.305), kind=kOutput, calls=%fused_computation.1 | convolution fusion | flops 134430720 | bytes 8814596 | tf_op jit(solution)/shard_map/while/body/eval_jaxpr/cond/branch_1_fun/dot_general | solution.py:76
  254.5 1.8 convolution_add_fusion
  256.3 13.4 %all_gather.13 = bf16[16,4096]{1,0:T(8,128)(2,1)S(1)} all-gather(bf16[16,1024]{1,0:T(8,128)(2,1)S(1)} %get-tuple-element.519), channel_id=1, replica_groups=mesh['section'=2,'dp'=4,'tensor'=4] {'tensor'}, dimensions={1}, use_global_device_ids=true | all-gather | bytes 163840 | tf_op jit(solution)/shard_map/while/body/eval_jaxpr/all_gather | solution.py:101
  269.7 2.4 conditional.7
  273.4 1.9 collective-permute-done
  275.3 2.3 multiply_convert_fusion.9
  278.6 7.4 %conditional.6 = (bf16[16,1024]{1,0:T(8,128)(2,1)S(1)}, f32[64,64]{1,0:T(8,128)}) conditional(s32[]{:T(128)} %convert_element_type.134, f32[64,64]{1,0:T(8,128)} %get-tuple-element.548, (bf16[16,4096]{1,0:T(8,128)(2,1)S(1)}, f32[128,4096]{1,0:T(8,128)S(1)}, s32[]{:T(128)}, bf16[1024,4096]{1,0:T(8,128)(2,1)}, bf16[128,64]{1,0:T(8,128)(2,1)}, ...), branch_computations={%region_3.3_spmd, %region_4.4_spmd} | conditional | flops 143152128 | bytes 10310676 | solution.py:95
  278.6 5.6 %convolution_convert_fusion = bf16[16,1024]{1,0:T(8,128)(2,1)S(1)} fusion(bf16[1024,4096]{1,0:T(8,128)(2,1)} %get-tuple-element.308, f32[128,4096]{1,0:T(8,128)S(1)} %get-tuple-element.306, s32[]{:T(128)} %get-tuple-element.307, bf16[16,4096]{1,0:T(8,128)(2,1)S(1)} %get-tuple-element.305), kind=kOutput, calls=%fused_computation.1 | convolution fusion | flops 134430720 | bytes 8814596 | tf_op jit(solution)/shard_map/while/body/eval_jaxpr/cond/branch_1_fun/dot_general | solution.py:76
  284.3 1.8 convolution_add_fusion
  286.0 13.4 %all_gather.13 = bf16[16,4096]{1,0:T(8,128)(2,1)S(1)} all-gather(bf16[16,1024]{1,0:T(8,128)(2,1)S(1)} %get-tuple-element.519), channel_id=1, replica_groups=mesh['section'=2,'dp'=4,'tensor'=4] {'tensor'}, dimensions={1}, use_global_device_ids=true | all-gather | bytes 163840 | tf_op jit(solution)/shard_map/while/body/eval_jaxpr/all_gather | solution.py:101
  299.4 2.4 conditional.7
  303.1 1.9 collective-permute-done
  305.0 2.3 multiply_convert_fusion.9
  308.3 7.4 %conditional.6 = (bf16[16,1024]{1,0:T(8,128)(2,1)S(1)}, f32[64,64]{1,0:T(8,128)}) conditional(s32[]{:T(128)} %convert_element_type.134, f32[64,64]{1,0:T(8,128)} %get-tuple-element.548, (bf16[16,4096]{1,0:T(8,128)(2,1)S(1)}, f32[128,4096]{1,0:T(8,128)S(1)}, s32[]{:T(128)}, bf16[1024,4096]{1,0:T(8,128)(2,1)}, bf16[128,64]{1,0:T(8,128)(2,1)}, ...), branch_computations={%region_3.3_spmd, %region_4.4_spmd} | conditional | flops 143152128 | bytes 10310676 | solution.py:95
  308.3 5.6 %convolution_convert_fusion = bf16[16,1024]{1,0:T(8,128)(2,1)S(1)} fusion(bf16[1024,4096]{1,0:T(8,128)(2,1)} %get-tuple-element.308, f32[128,4096]{1,0:T(8,128)S(1)} %get-tuple-element.306, s32[]{:T(128)} %get-tuple-element.307, bf16[16,4096]{1,0:T(8,128)(2,1)S(1)} %get-tuple-element.305), kind=kOutput, calls=%fused_computation.1 | convolution fusion | flops 134430720 | bytes 8814596 | tf_op jit(solution)/shard_map/while/body/eval_jaxpr/cond/branch_1_fun/dot_general | solution.py:76
  314.0 1.8 convolution_add_fusion
  315.8 13.4 %all_gather.13 = bf16[16,4096]{1,0:T(8,128)(2,1)S(1)} all-gather(bf16[16,1024]{1,0:T(8,128)(2,1)S(1)} %get-tuple-element.519), channel_id=1, replica_groups=mesh['section'=2,'dp'=4,'tensor'=4] {'tensor'}, dimensions={1}, use_global_device_ids=true | all-gather | bytes 163840 | tf_op jit(solution)/shard_map/while/body/eval_jaxpr/all_gather | solution.py:101
  329.1 2.4 conditional.7
  332.8 1.9 collective-permute-done
  334.8 2.3 multiply_convert_fusion.9
  338.0 7.4 %conditional.6 = (bf16[16,1024]{1,0:T(8,128)(2,1)S(1)}, f32[64,64]{1,0:T(8,128)}) conditional(s32[]{:T(128)} %convert_element_type.134, f32[64,64]{1,0:T(8,128)} %get-tuple-element.548, (bf16[16,4096]{1,0:T(8,128)(2,1)S(1)}, f32[128,4096]{1,0:T(8,128)S(1)}, s32[]{:T(128)}, bf16[1024,4096]{1,0:T(8,128)(2,1)}, bf16[128,64]{1,0:T(8,128)(2,1)}, ...), branch_computations={%region_3.3_spmd, %region_4.4_spmd} | conditional | flops 143152128 | bytes 10310676 | solution.py:95
  338.1 5.6 %convolution_convert_fusion = bf16[16,1024]{1,0:T(8,128)(2,1)S(1)} fusion(bf16[1024,4096]{1,0:T(8,128)(2,1)} %get-tuple-element.308, f32[128,4096]{1,0:T(8,128)S(1)} %get-tuple-element.306, s32[]{:T(128)} %get-tuple-element.307, bf16[16,4096]{1,0:T(8,128)(2,1)S(1)} %get-tuple-element.305), kind=kOutput, calls=%fused_computation.1 | convolution fusion | flops 134430720 | bytes 8814596 | tf_op jit(solution)/shard_map/while/body/eval_jaxpr/cond/branch_1_fun/dot_general | solution.py:76
  345.5 13.4 %all_gather.13 = bf16[16,4096]{1,0:T(8,128)(2,1)S(1)} all-gather(bf16[16,1024]{1,0:T(8,128)(2,1)S(1)} %get-tuple-element.519), channel_id=1, replica_groups=mesh['section'=2,'dp'=4,'tensor'=4] {'tensor'}, dimensions={1}, use_global_device_ids=true | all-gather | bytes 163840 | tf_op jit(solution)/shard_map/while/body/eval_jaxpr/all_gather | solution.py:101
  358.9 2.4 conditional.7
  362.5 1.9 collective-permute-done
  364.5 2.3 multiply_convert_fusion.9
  367.8 7.4 %conditional.6 = (bf16[16,1024]{1,0:T(8,128)(2,1)S(1)}, f32[64,64]{1,0:T(8,128)}) conditional(s32[]{:T(128)} %convert_element_type.134, f32[64,64]{1,0:T(8,128)} %get-tuple-element.548, (bf16[16,4096]{1,0:T(8,128)(2,1)S(1)}, f32[128,4096]{1,0:T(8,128)S(1)}, s32[]{:T(128)}, bf16[1024,4096]{1,0:T(8,128)(2,1)}, bf16[128,64]{1,0:T(8,128)(2,1)}, ...), branch_computations={%region_3.3_spmd, %region_4.4_spmd} | conditional | flops 143152128 | bytes 10310676 | solution.py:95
  367.8 5.6 %convolution_convert_fusion = bf16[16,1024]{1,0:T(8,128)(2,1)S(1)} fusion(bf16[1024,4096]{1,0:T(8,128)(2,1)} %get-tuple-element.308, f32[128,4096]{1,0:T(8,128)S(1)} %get-tuple-element.306, s32[]{:T(128)} %get-tuple-element.307, bf16[16,4096]{1,0:T(8,128)(2,1)S(1)} %get-tuple-element.305), kind=kOutput, calls=%fused_computation.1 | convolution fusion | flops 134430720 | bytes 8814596 | tf_op jit(solution)/shard_map/while/body/eval_jaxpr/cond/branch_1_fun/dot_general | solution.py:76
  375.2 13.4 %all_gather.13 = bf16[16,4096]{1,0:T(8,128)(2,1)S(1)} all-gather(bf16[16,1024]{1,0:T(8,128)(2,1)S(1)} %get-tuple-element.519), channel_id=1, replica_groups=mesh['section'=2,'dp'=4,'tensor'=4] {'tensor'}, dimensions={1}, use_global_device_ids=true | all-gather | bytes 163840 | tf_op jit(solution)/shard_map/while/body/eval_jaxpr/all_gather | solution.py:101
  388.6 2.4 conditional.7
  392.3 1.9 collective-permute-done
  394.2 2.3 multiply_convert_fusion.9
  397.5 7.4 %conditional.6 = (bf16[16,1024]{1,0:T(8,128)(2,1)S(1)}, f32[64,64]{1,0:T(8,128)}) conditional(s32[]{:T(128)} %convert_element_type.134, f32[64,64]{1,0:T(8,128)} %get-tuple-element.548, (bf16[16,4096]{1,0:T(8,128)(2,1)S(1)}, f32[128,4096]{1,0:T(8,128)S(1)}, s32[]{:T(128)}, bf16[1024,4096]{1,0:T(8,128)(2,1)}, bf16[128,64]{1,0:T(8,128)(2,1)}, ...), branch_computations={%region_3.3_spmd, %region_4.4_spmd} | conditional | flops 143152128 | bytes 10310676 | solution.py:95
  397.5 5.6 %convolution_convert_fusion = bf16[16,1024]{1,0:T(8,128)(2,1)S(1)} fusion(bf16[1024,4096]{1,0:T(8,128)(2,1)} %get-tuple-element.308, f32[128,4096]{1,0:T(8,128)S(1)} %get-tuple-element.306, s32[]{:T(128)} %get-tuple-element.307, bf16[16,4096]{1,0:T(8,128)(2,1)S(1)} %get-tuple-element.305), kind=kOutput, calls=%fused_computation.1 | convolution fusion | flops 134430720 | bytes 8814596 | tf_op jit(solution)/shard_map/while/body/eval_jaxpr/cond/branch_1_fun/dot_general | solution.py:76
  404.9 13.3 %all_gather.13 = bf16[16,4096]{1,0:T(8,128)(2,1)S(1)} all-gather(bf16[16,1024]{1,0:T(8,128)(2,1)S(1)} %get-tuple-element.519), channel_id=1, replica_groups=mesh['section'=2,'dp'=4,'tensor'=4] {'tensor'}, dimensions={1}, use_global_device_ids=true | all-gather | bytes 163840 | tf_op jit(solution)/shard_map/while/body/eval_jaxpr/all_gather | solution.py:101
  418.3 2.3 conditional.7
  421.9 1.9 collective-permute-done
  425.3 9.8 %psum.22 = f32[2,1024]{1,0:T(2,128)S(1)} all-reduce(f32[2,1024]{1,0:T(2,128)S(1)} %broadcast_multiply_fusion.1), channel_id=1, replica_groups=mesh['section'=2,'dp'=4,'tensor'=4] {'dp'}, use_global_device_ids=true, to_apply=%region_9.10 | all-reduce | flops 2048 | bytes 16384 | tf_op jit(solution)/shard_map/psum | solution.py:131
  435.3 14.3 %psum.23 = f32[2,64]{1,0:T(2,128)} all-reduce(f32[2,64]{1,0:T(2,128)S(1)} %fusion.32), channel_id=1, replica_groups=mesh['section'=2,'dp'=4,'tensor'=4] {'section','tensor'}, use_global_device_ids=true, to_apply=%region_10.11 | all-reduce | flops 128 | bytes 1024 | tf_op jit(solution)/shard_map/psum | solution.py:134
  (103 shorter events, 53.5 us)
Async XLA Ops:
  7.2 428.0 %copy-start = (bf16[1,64,1024]{2,1,0:T(8,128)(2,1)S(1)}, bf16[1,64,1024]{2,1,0:T(8,128)(2,1)}, u32[]{:S(2)}) copy-start(bf16[1,64,1024]{2,1,0:T(8,128)(2,1)} %param.17) | copy-start | bytes 393220
  7.2 1.3 copy-start.1
  7.2 2.1 copy-start.2
  7.2 92.9 %all-gather.3.cloned.1.call-start = ((), (), s32[]{:S(2)}) async-start(), calls=%async_computation.1 | async-start | bytes 10485760 | tf_op jit(solution)/shard_map/all_gather | solution.py:55
  7.9 149.9 %all-reduce.2.cloned.1.call-start = ((), (), s32[]{:S(2)}) async-start(), calls=%async_computation | async-start | bytes 2097152 | tf_op jit(solution)/shard_map/psum | solution.py:58
  100.1 5.7 %copy-start.4 = (s32[1,2]{1,0:T(1,128)S(1)}, s32[1,2]{1,0:T(1,128)}, u32[]{:S(2)}) copy-start(s32[1,2]{1,0:T(1,128)} %param.15) | copy-start | bytes 28
  163.7 13.4 %copy-start.5 = (f32[128,1]{0,1:T(1,128)S(1)}, f32[128,1]{0,1:T(1,128)}, u32[]{:S(2)}) copy-start(f32[128,1]{0,1:T(1,128)} %get-tuple-element.578) | copy-start | bytes 1540 | tf_op jit(solution)/shard_map/while
  177.1 8.9 %collective-permute-start = (bf16[16,4096]{1,0:T(8,128)(2,1)S(1)}, bf16[16,4096]{1,0:T(8,128)(2,1)S(1)}, u32[]{:S(2)}, u32[]{:S(2)}) collective-permute-start(bf16[16,4096]{1,0:T(8,128)(2,1)S(1)} %get-tuple-element.588), channel_id=1, source_target_pairs={{16,0},{17,1},{18,2},{19,3},{20,4},{21,5},{22,6},{23,7},{24,8},{25... | collective-permute-start | bytes 393224 | tf_op jit(solution)/shard_map/while/body/eval_jaxpr/ppermute | solution.py:19
  189.3 20.9 %copy-start.5 = (f32[128,1]{0,1:T(1,128)S(1)}, f32[128,1]{0,1:T(1,128)}, u32[]{:S(2)}) copy-start(f32[128,1]{0,1:T(1,128)} %get-tuple-element.578) | copy-start | bytes 1540 | tf_op jit(solution)/shard_map/while
  212.6 3.2 collective-permute-start
  219.1 20.8 %copy-start.5 = (f32[128,1]{0,1:T(1,128)S(1)}, f32[128,1]{0,1:T(1,128)}, u32[]{:S(2)}) copy-start(f32[128,1]{0,1:T(1,128)} %get-tuple-element.578) | copy-start | bytes 1540 | tf_op jit(solution)/shard_map/while
  242.3 3.2 collective-permute-start
  248.9 20.8 %copy-start.5 = (f32[128,1]{0,1:T(1,128)S(1)}, f32[128,1]{0,1:T(1,128)}, u32[]{:S(2)}) copy-start(f32[128,1]{0,1:T(1,128)} %get-tuple-element.578) | copy-start | bytes 1540 | tf_op jit(solution)/shard_map/while
  272.1 3.2 collective-permute-start
  278.6 20.8 %copy-start.5 = (f32[128,1]{0,1:T(1,128)S(1)}, f32[128,1]{0,1:T(1,128)}, u32[]{:S(2)}) copy-start(f32[128,1]{0,1:T(1,128)} %get-tuple-element.578) | copy-start | bytes 1540 | tf_op jit(solution)/shard_map/while
  301.8 3.2 collective-permute-start
  308.3 20.8 %copy-start.5 = (f32[128,1]{0,1:T(1,128)S(1)}, f32[128,1]{0,1:T(1,128)}, u32[]{:S(2)}) copy-start(f32[128,1]{0,1:T(1,128)} %get-tuple-element.578) | copy-start | bytes 1540 | tf_op jit(solution)/shard_map/while
  331.5 3.2 collective-permute-start
  338.0 20.8 %copy-start.5 = (f32[128,1]{0,1:T(1,128)S(1)}, f32[128,1]{0,1:T(1,128)}, u32[]{:S(2)}) copy-start(f32[128,1]{0,1:T(1,128)} %get-tuple-element.578) | copy-start | bytes 1540 | tf_op jit(solution)/shard_map/while
  361.2 3.2 collective-permute-start
  367.8 20.8 %copy-start.5 = (f32[128,1]{0,1:T(1,128)S(1)}, f32[128,1]{0,1:T(1,128)}, u32[]{:S(2)}) copy-start(f32[128,1]{0,1:T(1,128)} %get-tuple-element.578) | copy-start | bytes 1540 | tf_op jit(solution)/shard_map/while
  391.0 3.2 collective-permute-start
  397.5 20.8 %copy-start.5 = (f32[128,1]{0,1:T(1,128)S(1)}, f32[128,1]{0,1:T(1,128)}, u32[]{:S(2)}) copy-start(f32[128,1]{0,1:T(1,128)} %get-tuple-element.578) | copy-start | bytes 1540 | tf_op jit(solution)/shard_map/while
  420.5 3.2 collective-permute-start
  435.2 14.5 %copy-start.3 = (f32[2,1024]{1,0:T(2,128)}, f32[2,1024]{1,0:T(2,128)S(1)}, u32[]{:S(2)}) copy-start(f32[2,1024]{1,0:T(2,128)S(1)} %psum.22) | copy-start | bytes 24580
Sparse Core Ops, SparseCore 0:
  9.9 90.1 all-gather.2
  105.9 51.8 all-reduce.1
where the time goes:
time: 461 us; the launch traced here: 456 us
  waiting for transfers between devices  158 us (34%)
  blocking collectives  144 us (31%)
  matrix products  67.3 us (15%)
  other arithmetic  54.6 us (12%)
  between operations  15.4 us (3%)
  starting transfers between devices  11.7 us (3%)
    all_gather x9, blocking collectives, turn(): full_grads = lax.all_gather(own_grads, 'tensor', axis=1, tiled=True)  120 us
    all_gather x1, waiting for transfers between devices, body(): weight_rows = lax.all_gather(weights[0], 'dp', axis=1, tiled=True)  89.1 us
    psum x1, waiting for transfers between devices, body(): lax.psum(partial_value.astype(jnp.bfloat16), 'tensor').astype(jnp.float32)  45.6 us
    dot_general x8, matrix products, block_grad(): lax.dot_general(grad_pre, weight_rows, (((1,), (1,)), ((), ())), preferre...  45.2 us
    ppermute x9, waiting for transfers between devices, passed_along(): lax.ppermute(value, axis, [(source, source + steps) for source in range(f...  23.1 us
    convert_element_type x9, other arithmetic, sign_table(): (jnp.where(parity == 1, 1.0, -1.0) * (1.0 / math.sqrt(row_count))).astype...  21 us
    psum x1, blocking collectives, body(): scores = lax.psum(partial_scores, ('section', 'tensor'))  14.3 us
    dot_general x8, matrix products, block_grad(): lax.dot_general(feature_rows, out_features, (((0,), (0,)), ((), ())), pre...  14.2 us
  transfers between devices with their start and end apart: 11, of which 11 were waited for; matrix products, arithmetic and copies ran while one was open for 2% of the time, Pallas kernels for 0%

commit v1 on v0

v1 whole, which is shorter than its diff:
```python
import functools
import math

import jax
import jax.numpy as jnp
from jax import lax
from jax.experimental import pallas as pl
from jax.experimental.pallas import tpu as pltpu
from jax.sharding import PartitionSpec as P

R = 64
SEQS = 2
eps = 1e-05
F32 = jnp.float32
BF16 = jnp.bfloat16
MESH = pl.DeviceIdType.MESH
NT = (((1,), (1,)), ((), ()))


def sign_rows(seed_value, row_start, row_count, scale):
    row_index = lax.broadcasted_iota(jnp.int32, (R, row_count), 1) + row_start
    col_index = lax.broadcasted_iota(jnp.int32, (R, row_count), 0)
    mixing = row_index * 40503 + col_index * 9973 + (seed_value * 7919 + 12345)
    mixing = mixing ^ (mixing >> 13)
    mixing = mixing * 1274126177
    mixing = mixing ^ (mixing >> 16)
    parity = (mixing >> 10) & 1
    return jnp.where(parity == 1, scale, -scale).astype(BF16)


def kernel(
    sections, nd, nz,
    x_ref, w_ref, gain_ref, seed_ref, og_ref, q_ref,
    grads_ref, scores_ref,
    a_buf, inf_buf, ps_buf, pr_buf, slope_buf, ui_buf, uii_buf, gp_buf,
    gns_buf, gnr_buf, dot_buf, up_buf, g_buf, gr_buf, sc_buf,
    a_ss, a_rs, inf_ss, inf_rs, p_ss, p_rs, og_ss, og_rs, gp_ss, gp_rs,
    gn_ss, gn_rs, dt_ss, dt_rs, up_ss, up_rs, uii_ss, uii_rs,
    g_ss, g_rs, sc_ss, sc_rs,
):
    s = lax.axis_index("section")
    d = lax.axis_index("dp")
    z = lax.axis_index("tensor")
    tok, width = x_ref.shape
    feat = width // nz
    cols = width // nd
    sub = tok // nz
    at_top = s == sections - 1
    lower = s > 0
    z_start = pl.multiple_of(z * feat, feat)
    d_start = pl.multiple_of(d * cols, cols)
    sub_start = pl.multiple_of(z * sub, sub)

    def dev(s_to, d_to, z_to):
        return {"section": s_to, "dp": d_to, "tensor": z_to}

    def remote(src, dst, ss, rs, to):
        return pltpu.make_async_remote_copy(
            src_ref=src, dst_ref=dst, send_sem=ss, recv_sem=rs, device_id=to, device_id_type=MESH
        )

    barrier = pltpu.get_barrier_semaphore()
    total = sections * nd * nz
    me = (s * nd + d) * nz + z

    @pl.loop(1, total)
    def _(step):
        other = lax.rem(me + step, total)
        pl.semaphore_signal(
            barrier, inc=1, device_id_type=MESH,
            device_id=dev(other // (nd * nz), lax.rem(other // nz, nd), lax.rem(other, nz)),
        )

    hidden = x_ref[...].astype(F32)
    radius = jnp.sqrt(jnp.mean(hidden * hidden, axis=1, keepdims=True) + eps)
    gain_z = gain_ref[:, pl.ds(z_start, feat)]
    normed_z = x_ref[:, pl.ds(z_start, feat)].astype(F32) / radius
    a_buf[d] = (normed_z * gain_z).astype(BF16)

    pl.semaphore_wait(barrier, total - 1)

    def a_copy(o):
        to = lax.rem(d + o, nd)
        return remote(a_buf.at[d], a_buf.at[d], a_ss.at[o], a_rs.at[o], dev(s, to, z))

    for o in range(1, nd):
        a_copy(o).start()

    def og_copy(o):
        to = lax.rem(d + o, nd)
        src = og_ref.at[pl.ds(sub_start, sub), pl.ds(pl.multiple_of(to * cols, cols), cols)]
        return remote(src, ui_buf.at[d], og_ss.at[o], og_rs.at[o], dev(s, to, z))

    @pl.when(at_top)
    def _():
        for o in range(1, nd):
            og_copy(o).start()
        ui_buf[d] = og_ref[pl.ds(sub_start, sub), pl.ds(d_start, cols)]

    scale = 1.0 / math.sqrt(width)
    x_sub = x_ref[pl.ds(sub_start, sub), :].astype(F32)
    radius_sub = jnp.sqrt(jnp.mean(x_sub * x_sub, axis=1, keepdims=True) + eps)
    lifted_sub = (x_sub / radius_sub * gain_ref[...]).astype(BF16)
    table_in = sign_rows(seed_ref[0, 0], 0, width, scale)
    inf_buf[d] = lax.dot_general(lifted_sub, table_in, NT, preferred_element_type=F32)

    def inf_copy(o):
        to = lax.rem(d + o, nd)
        return remote(inf_buf.at[d], inf_buf.at[d], inf_ss.at[o], inf_rs.at[o], dev(s, to, z))

    for o in range(1, nd):
        inf_copy(o).start()

    for o in range(nd):
        block = lax.rem(d + nd - o, nd)
        if o:
            a_copy(o).wait_recv()
        part = jnp.dot(a_buf[block], w_ref[...], preferred_element_type=F32).astype(BF16)
        for zt in range(nz):
            ps_buf[zt, block] = part[zt * sub : (zt + 1) * sub, :]

    def p_copy(o):
        to = lax.rem(z + o, nz)
        return remote(ps_buf.at[to], pr_buf.at[z], p_ss.at[o], p_rs.at[o], dev(s, d, to))

    for o in range(1, nz):
        p_copy(o).start()
    pr_buf[z] = ps_buf[z]
    table_out = sign_rows(seed_ref[0, 1], d_start, cols, scale)
    for o in range(1, nz):
        p_copy(o).wait_recv()
    summed = pr_buf[0].astype(F32)
    for zt in range(1, nz):
        summed = summed + pr_buf[zt].astype(F32)
    sig = jax.nn.sigmoid(summed)
    slope_buf[...] = sig * (1.0 + summed * (1.0 - sig))

    def up_copy(zt, source):
        return remote(
            up_buf.at[pl.ds(zt * sub, sub)], ui_buf.at[source], up_ss.at[zt], up_rs.at[source],
            dev(jnp.maximum(s - 1, 0), z, zt),
        )

    def uii_copy():
        return remote(up_buf, uii_buf, uii_ss.at[0], uii_rs.at[0], dev(jnp.maximum(s - 1, 0), d, z))

    @pl.when(at_top)
    def _():
        for o in range(1, nd):
            og_copy(o).wait_recv()
        uii_buf[...] = og_ref[:, pl.ds(z_start, feat)]

    @pl.when(jnp.logical_not(at_top))
    def _():
        for source in range(nd):
            up_copy(0, source).wait_recv()

    grad_pre = (ui_buf[...].astype(F32) * slope_buf[...]).astype(BF16)
    gp_buf[z] = grad_pre

    def gp_copy(o):
        to = lax.rem(z + o, nz)
        return remote(gp_buf.at[z], gp_buf.at[z], gp_ss.at[o], gp_rs.at[o], dev(s, d, to))

    @pl.when(lower)
    def _():
        for o in range(1, nz):
            gp_copy(o).start()

    for o in range(1, nd):
        inf_copy(o).wait_recv()
    out_feat = lax.dot_general(
        grad_pre.reshape(nd * sub, cols), table_out, NT, preferred_element_type=F32
    ).astype(BF16)
    in_feat = inf_buf[...].reshape(nd * sub, R).astype(BF16)
    piece = R * R // nz
    per_seq = nd * sub // SEQS
    for zt in range(nz):
        entry = lax.broadcasted_iota(jnp.int32, (R, piece), 1) + zt * piece
        which = lax.broadcasted_iota(jnp.int32, (R, piece), 0)
        pick_in = (entry // R == which).astype(F32).astype(BF16)
        pick_out = (entry % R == which).astype(F32).astype(BF16)
        left = jnp.dot(in_feat, pick_in, preferred_element_type=F32)
        right = jnp.dot(out_feat, pick_out, preferred_element_type=F32)
        product = left * right
        for k in range(SEQS):
            g_buf[zt, k : k + 1, :] = jnp.sum(
                product[k * per_seq : (k + 1) * per_seq], axis=0, keepdims=True
            )

    plane = nd * nz
    mine = d * nz + z

    def g_copy(o):
        to = lax.rem(mine + o, plane)
        return remote(
            g_buf.at[lax.rem(to, nz)], gr_buf.at[mine], g_ss.at[o], g_rs.at[o],
            dev(s, to // nz, lax.rem(to, nz)),
        )

    for o in range(1, plane):
        g_copy(o).start()
    gr_buf[mine] = g_buf[z]

    def gn_copy(o):
        to = lax.rem(d + o, nd)
        return remote(gns_buf.at[to], gnr_buf.at[d], gn_ss.at[o], gn_rs.at[o], dev(s, to, z))

    def dt_copy(o):
        to = lax.rem(z + o, nz)
        return remote(dot_buf.at[z], dot_buf.at[z], dt_ss.at[o], dt_rs.at[o], dev(s, d, to))

    @pl.when(lower)
    def _():
        for o in range(nz):
            block = lax.rem(z + nz - o, nz)
            if o:
                gp_copy(o).wait_recv()
            rows = gp_buf[block].reshape(nd * sub, cols)
            part = lax.dot_general(rows, w_ref[...], NT, preferred_element_type=F32).astype(BF16)
            for dt in range(nd):
                gns_buf[dt, block] = part[dt * sub : (dt + 1) * sub, :]
        for o in range(1, nd):
            gn_copy(o).start()
        gnr_buf[d] = gns_buf[d]
        for o in range(1, nd):
            gn_copy(o).wait_recv()
        grad_norm = gnr_buf[0].astype(F32)
        for dt in range(1, nd):
            grad_norm = grad_norm + gnr_buf[dt].astype(F32)
        grad_norm = grad_norm.astype(BF16).astype(F32).reshape(tok, feat)
        scaled = grad_norm * gain_ref[:, pl.ds(z_start, feat)]
        x_z = x_ref[:, pl.ds(z_start, feat)].astype(F32)
        x_all = x_ref[...].astype(F32)
        rad = jnp.sqrt(jnp.mean(x_all * x_all, axis=1, keepdims=True) + eps)
        normed = x_z / rad
        own_dot = jnp.sum(scaled * normed, axis=1, keepdims=True)
        dot_buf[z] = jnp.broadcast_to(own_dot, (tok, tok)).T[:8, :]
        for o in range(1, nz):
            dt_copy(o).start()
        if sections > 2:
            @pl.when(jnp.logical_not(at_top))
            def _():
                uii_copy().wait_recv()
        for o in range(1, nz):
            dt_copy(o).wait_recv()
        dots = dot_buf[0]
        for zt in range(1, nz):
            dots = dots + dot_buf[zt]
        mean_dot = jnp.broadcast_to(dots[:1, :], (tok, tok)).T[:, :1] * (1.0 / width)
        up_buf[...] = (uii_buf[...].astype(F32) + (scaled - normed * mean_dot) / rad).astype(BF16)
        for zt in range(nz):
            up_copy(zt, d).start()
        if sections > 2:
            @pl.when(s > 1)
            def _():
                uii_copy().start()

    for o in range(1, plane):
        g_copy(o).wait_recv()
    grads = gr_buf[0]
    for other in range(1, plane):
        grads = grads + gr_buf[other]
    grads_ref[...] = grads
    queries = q_ref[...]
    high = grads.astype(BF16)
    rest = grads - high.astype(F32)
    middle = rest.astype(BF16)
    low = (rest - middle.astype(F32)).astype(BF16)
    part = lax.dot_general(high, queries, NT, preferred_element_type=F32)
    part = part + lax.dot_general(middle, queries, NT, preferred_element_type=F32)
    part = part + lax.dot_general(low, queries, NT, preferred_element_type=F32)
    column = sections * nz
    here = s * nz + z
    sc_buf[here] = part

    def sc_copy(o):
        to = lax.rem(here + o, column)
        return remote(
            sc_buf.at[here], sc_buf.at[here], sc_ss.at[o], sc_rs.at[o],
            dev(to // nz, d, lax.rem(to, nz)),
        )

    for o in range(1, column):
        sc_copy(o).start()

    for o in range(1, nd):
        a_copy(o).wait_send()
        inf_copy(o).wait_send()
    for o in range(1, nz):
        p_copy(o).wait_send()

    @pl.when(at_top)
    def _():
        for o in range(1, nd):
            og_copy(o).wait_send()

    @pl.when(lower)
    def _():
        for o in range(1, nz):
            gp_copy(o).wait_send()
            dt_copy(o).wait_send()
        for o in range(1, nd):
            gn_copy(o).wait_send()
        for zt in range(nz):
            up_copy(zt, d).wait_send()
        if sections > 2:
            @pl.when(s > 1)
            def _():
                uii_copy().wait_send()

    for o in range(1, plane):
        g_copy(o).wait_send()
    for o in range(1, column):
        sc_copy(o).wait_recv()
    scores = sc_buf[0]
    for other in range(1, column):
        scores = scores + sc_buf[other]
    scores_ref[...] = scores
    for o in range(1, column):
        sc_copy(o).wait_send()


def body(section_input, weights, gains, proj_seeds, out_grad, query_grads):
    sections = lax.axis_size("section")
    nd = lax.axis_size("dp")
    nz = lax.axis_size("tensor")
    tok, width = section_input.shape[1:]
    feat = weights.shape[1]
    cols = weights.shape[2]
    assert nd == nz and feat == cols
    sub = tok // nz
    piece = R * R // nz
    queries = query_grads.shape[1]
    column = sections * nz
    plane = nd * nz
    vmem = pl.BlockSpec(memory_space=pltpu.VMEM)
    dma = pltpu.SemaphoreType.DMA
    sems = []
    for count in (nd, nd, nz, nd, nz, nd, nz):
        sems += [dma((count,)), dma((count,))]
    sems += [dma((nz,)), dma((nd,)), dma((1,)), dma((1,))]
    sems += [dma((plane,)), dma((plane,)), dma((column,)), dma((column,))]
    grads, scores = pl.pallas_call(
        functools.partial(kernel, sections, nd, nz),
        out_shape=(
            jax.ShapeDtypeStruct((SEQS, piece), F32),
            jax.ShapeDtypeStruct((SEQS, queries), F32),
        ),
        in_specs=[vmem, vmem, vmem, pl.BlockSpec(memory_space=pltpu.SMEM), vmem, vmem],
        out_specs=(vmem, vmem),
        scratch_shapes=[
            pltpu.VMEM((nd, tok, feat), BF16),
            pltpu.VMEM((nd, sub, R), F32),
            pltpu.VMEM((nz, nd, sub, cols), BF16),
            pltpu.VMEM((nz, nd, sub, cols), BF16),
            pltpu.VMEM((nd, sub, cols), F32),
            pltpu.VMEM((nd, sub, cols), BF16),
            pltpu.VMEM((tok, feat), BF16),
            pltpu.VMEM((nz, nd, sub, cols), BF16),
            pltpu.VMEM((nd, nz, sub, feat), BF16),
            pltpu.VMEM((nd, nz, sub, feat), BF16),
            pltpu.VMEM((nz, 8, tok), F32),
            pltpu.VMEM((tok, feat), BF16),
            pltpu.VMEM((nz, SEQS, piece), F32),
            pltpu.VMEM((plane, SEQS, piece), F32),
            pltpu.VMEM((column, SEQS, queries), F32),
            *sems,
        ],
        compiler_params=pltpu.CompilerParams(
            collective_id=0, has_side_effects=True, vmem_limit_bytes=60 * 1024 * 1024
        ),
    )(section_input[0], weights[0], gains, proj_seeds, out_grad, query_grads[0])
    return (grads[None], scores)


def solution(mesh):
    in_specs = (
        P("section", "dp", None),
        P("section", "tensor", "dp"),
        P("section", None),
        P("section", None),
        P("dp", None),
        P("section", "dp", "tensor"),
    )
    out_specs = (P("section", None, "tensor"), P(None, "dp"))
    return jax.shard_map(body, mesh=mesh, in_specs=in_specs, out_specs=out_specs, check_vma=False)
```

time: 461 us -> 91.1 us (0.20)
  waiting for transfers between devices: 158 us -> 0 us
  blocking collectives: 144 us -> 0 us
  Pallas kernels: 0 us -> 87.7 us
  matrix products: 67.3 us -> 0 us
  other arithmetic: 54.6 us -> 0 us
  between operations: 15.4 us -> 0.64 us
  starting transfers between devices: 11.7 us -> 0 us
    all_gather x9 -> x0, blocking collectives: 120 us -> none  [turn(): full_grads = lax.all_gather(own_grads, 'tensor', axis=1, tiled=True)]
    all_gather x1 -> x0, waiting for transfers between devices: 89.1 us -> none  [body(): weight_rows = lax.all_gather(weights[0], 'dp', axis=1, tiled=True)]
    pallas_call x0 -> x1, Pallas kernels: none -> 87.7 us  [body(): pl.pallas_call(functools.partial(kernel, sections, nd, nz), out_shape=(ja...]
    dot_general x19 -> x0, matrix products: 67.3 us -> none  [the longest x8 45.2 us: block_grad(): lax.dot_general(grad_pre, weight_rows, (((1,), (1,)), ((), ())), preferre...]
    psum x1 -> x0, waiting for transfers between devices: 45.6 us -> none  [body(): lax.psum(partial_value.astype(jnp.bfloat16), 'tensor').astype(jnp.float32)]
    convert_element_type x18 -> x0, other arithmetic: 30.4 us -> none  [the longest x9 21 us: sign_table(): (jnp.where(parity == 1, 1.0, -1.0) * (1.0 / math.sqrt(row_count))).astype...]
    psum x2 -> x0, blocking collectives: 24.1 us -> none  [the longest x1 14.3 us: body(): scores = lax.psum(partial_scores, ('section', 'tensor'))]
    ppermute x9 -> x0, waiting for transfers between devices: 23.1 us -> none  [passed_along(): lax.ppermute(value, axis, [(source, source + steps) for source in range(f...]
  transfers between devices with their start and end apart: 11 -> 0, of which waited for: 11 -> 0; matrix products, arithmetic and copies ran while one was open for 2% -> 0% of each run, Pallas kernels for 0% -> 0%
where the time goes in v1:
time: 91.1 us; the launch traced here: 90.9 us
  Pallas kernels  87.7 us (96%)
  local copies, waits for them, and re-layouts  2.51 us (3%)
    pallas_call x1, Pallas kernels, body(): pl.pallas_call(functools.partial(kernel, sections, nd, nz), out_shape=(ja...  87.7 us
    unnamed x2, local copies, waits for them, and re-layouts  2.51 us

profile of v1, /device:TPU:0, one launch (start us, length us, event | category | flops | bytes accessed | tf_op | source)
XLA Modules:
  0.0 90.9 jit_solution(3913593532901022033)
XLA Ops:
  0.6 87.7 %shard_map.77 = (f32[2,1024]{1,0:T(2,128)}, f32[2,64]{1,0:T(2,128)}) custom-call(bf16[128,4096]{1,0:T(8,128)(2,1)} %bitcast.5, bf16[1024,1024]{1,0:T(8,128)(2,1)} %bitcast.4, f32[1,4096]{1,0:T(1,128)} %gain_ref.1, s32[1,2]{1,0:T(1,128)} %seed_ref.1, bf16[128,4096]{1,0:T(8,128)(2,1)} %og_ref.1, bf16[64,1024]{1,0:T(8,128)(2,1)} %bitcast.6), custom_call_target="tpu_custom_call" | custom-call | tf_op jit(solution)/shard_map/pallas_call | solution.py:344
  88.4 1.3 %copy.10 = f32[1,2,1024]{2,1,0:T(2,128)} copy(f32[1,2,1024]{2,1,0:T(2,128)} %bitcast.7) | data formatting | bytes 16384
  89.7 1.2 %copy.11 = f32[2,64]{1,0:T(2,128)} copy(f32[2,64]{1,0:T(2,128)} %get-tuple-element.9) | data formatting | bytes 1024

commit v2 on v1

--- a/solution.py
+++ b/solution.py
@@ -30,26 +30,29 @@
 
 def kernel(
     sections, nd, nz,
-    x_ref, w_ref, gain_ref, seed_ref, og_ref, q_ref,
+    x_hbm, w_hbm, gain_ref, seed_ref, og_ref, q_ref,
     grads_ref, scores_ref,
     a_buf, inf_buf, ps_buf, pr_buf, slope_buf, ui_buf, uii_buf, gp_buf,
     gns_buf, gnr_buf, dot_buf, up_buf, g_buf, gr_buf, sc_buf,
+    x_ref, w_ref, sum_buf, norm_buf, rad_buf, turn_buf, mean_buf,
     a_ss, a_rs, inf_ss, inf_rs, p_ss, p_rs, og_ss, og_rs, gp_ss, gp_rs,
     gn_ss, gn_rs, dt_ss, dt_rs, up_ss, up_rs, uii_ss, uii_rs,
-    g_ss, g_rs, sc_ss, sc_rs,
+    g_ss, g_rs, sc_ss, sc_rs, in_sem, go_sem,
 ):
     s = lax.axis_index("section")
     d = lax.axis_index("dp")
     z = lax.axis_index("tensor")
-    tok, width = x_ref.shape
+    tok, width = x_hbm.shape
     feat = width // nz
     cols = width // nd
     sub = tok // nz
     at_top = s == sections - 1
+    below_top = s == sections - 2
     lower = s > 0
     z_start = pl.multiple_of(z * feat, feat)
     d_start = pl.multiple_of(d * cols, cols)
     sub_start = pl.multiple_of(z * sub, sub)
+    sub_start_d = pl.multiple_of(d * sub, sub)
 
     def dev(s_to, d_to, z_to):
         return {"section": s_to, "dp": d_to, "tensor": z_to}
@@ -58,6 +61,11 @@
         return pltpu.make_async_remote_copy(
             src_ref=src, dst_ref=dst, send_sem=ss, recv_sem=rs, device_id=to, device_id_type=MESH
         )
+
+    x_load = pltpu.make_async_copy(x_hbm, x_ref, in_sem.at[0])
+    w_load = pltpu.make_async_copy(w_hbm, w_ref, in_sem.at[1])
+    x_load.start()
+    w_load.start()
 
     barrier = pltpu.get_barrier_semaphore()
     total = sections * nd * nz
@@ -71,10 +79,13 @@
             device_id=dev(other // (nd * nz), lax.rem(other // nz, nd), lax.rem(other, nz)),
         )
 
+    x_load.wait()
     hidden = x_ref[...].astype(F32)
     radius = jnp.sqrt(jnp.mean(hidden * hidden, axis=1, keepdims=True) + eps)
     gain_z = gain_ref[:, pl.ds(z_start, feat)]
     normed_z = x_ref[:, pl.ds(z_start, feat)].astype(F32) / radius
+    norm_buf[...] = normed_z
+    rad_buf[...] = jnp.broadcast_to(radius, rad_buf.shape)
     a_buf[d] = (normed_z * gain_z).astype(BF16)
 
     pl.semaphore_wait(barrier, total - 1)
@@ -83,19 +94,29 @@
         to = lax.rem(d + o, nd)
         return remote(a_buf.at[d], a_buf.at[d], a_ss.at[o], a_rs.at[o], dev(s, to, z))
 
-    for o in range(1, nd):
-        a_copy(o).start()
+    @pl.when(jnp.logical_not(below_top))
+    def _():
+        for o in range(1, nd):
+            a_copy(o).start()
 
     def og_copy(o):
         to = lax.rem(d + o, nd)
         src = og_ref.at[pl.ds(sub_start, sub), pl.ds(pl.multiple_of(to * cols, cols), cols)]
         return remote(src, ui_buf.at[d], og_ss.at[o], og_rs.at[o], dev(s, to, z))
 
+    def ui_load():
+        src = og_ref.at[pl.ds(sub_start, sub), pl.ds(d_start, cols)]
+        return pltpu.make_async_copy(src, ui_buf.at[d], in_sem.at[2])
+
+    def uii_load():
+        return pltpu.make_async_copy(og_ref.at[:, pl.ds(z_start, feat)], uii_buf, in_sem.at[3])
+
     @pl.when(at_top)
     def _():
         for o in range(1, nd):
             og_copy(o).start()
-        ui_buf[d] = og_ref[pl.ds(sub_start, sub), pl.ds(d_start, cols)]
+        ui_load().start()
+        uii_load().start()
 
     scale = 1.0 / math.sqrt(width)
     x_sub = x_ref[pl.ds(sub_start, sub), :].astype(F32)
@@ -111,6 +132,13 @@
     for o in range(1, nd):
         inf_copy(o).start()
 
+    @pl.when(below_top)
+    def _():
+        pl.semaphore_wait(go_sem.at[0], 1)
+        for o in range(1, nd):
+            a_copy(o).start()
+
+    w_load.wait()
     for o in range(nd):
         block = lax.rem(d + nd - o, nd)
         if o:
@@ -118,6 +146,23 @@
         part = jnp.dot(a_buf[block], w_ref[...], preferred_element_type=F32).astype(BF16)
         for zt in range(nz):
             ps_buf[zt, block] = part[zt * sub : (zt + 1) * sub, :]
+
+    for o in range(1, nd):
+        a_copy(o).wait_send()
+
+    def go(which):
+        pl.semaphore_signal(
+            go_sem.at[which], inc=1, device_id=dev(jnp.maximum(s - 1, 0), d, z), device_id_type=MESH
+        )
+
+    if sections > 1:
+        @pl.when(at_top)
+        def _():
+            go(0)
+
+        @pl.when(below_top)
+        def _():
+            pl.semaphore_wait(go_sem.at[1], 1)
 
     def p_copy(o):
         to = lax.rem(z + o, nz)
@@ -133,6 +178,7 @@
     for zt in range(1, nz):
         summed = summed + pr_buf[zt].astype(F32)
     sig = jax.nn.sigmoid(summed)
+    sum_buf[...] = summed
     slope_buf[...] = sig * (1.0 + summed * (1.0 - sig))
 
     def up_copy(zt, source):
@@ -148,7 +194,8 @@
     def _():
         for o in range(1, nd):
             og_copy(o).wait_recv()
-        uii_buf[...] = og_ref[:, pl.ds(z_start, feat)]
+        ui_load().wait()
+        uii_load().wait()
 
     @pl.when(jnp.logical_not(at_top))
     def _():
@@ -162,10 +209,25 @@
         to = lax.rem(z + o, nz)
         return remote(gp_buf.at[z], gp_buf.at[z], gp_ss.at[o], gp_rs.at[o], dev(s, d, to))
 
+    plane = nd * nz
+    mine = d * nz + z
+
+    def dt_copy(o):
+        to = lax.rem(mine + o, plane)
+        return remote(
+            dot_buf.at[mine], dot_buf.at[mine], dt_ss.at[o], dt_rs.at[o],
+            dev(s, to // nz, lax.rem(to, nz)),
+        )
+
     @pl.when(lower)
     def _():
         for o in range(1, nz):
             gp_copy(o).start()
+        pre = gp_buf[z].astype(F32) * sum_buf[...]
+        own_dot = jnp.sum(pre.reshape(nd * sub, cols), axis=1, keepdims=True)
+        dot_buf[mine] = jnp.broadcast_to(own_dot, (tok, tok)).T[:8, :]
+        for o in range(1, plane):
+            dt_copy(o).start()
 
     for o in range(1, nd):
         inf_copy(o).wait_recv()
@@ -188,9 +250,6 @@
                 product[k * per_seq : (k + 1) * per_seq], axis=0, keepdims=True
             )
 
-    plane = nd * nz
-    mine = d * nz + z
-
     def g_copy(o):
         to = lax.rem(mine + o, plane)
         return remote(
@@ -205,10 +264,6 @@
     def gn_copy(o):
         to = lax.rem(d + o, nd)
         return remote(gns_buf.at[to], gnr_buf.at[d], gn_ss.at[o], gn_rs.at[o], dev(s, to, z))
-
-    def dt_copy(o):
-        to = lax.rem(z + o, nz)
-        return remote(dot_buf.at[z], dot_buf.at[z], dt_ss.at[o], dt_rs.at[o], dev(s, d, to))
 
     @pl.when(lower)
     def _():
@@ -220,9 +275,24 @@
             part = lax.dot_general(rows, w_ref[...], NT, preferred_element_type=F32).astype(BF16)
             for dt in range(nd):
                 gns_buf[dt, block] = part[dt * sub : (dt + 1) * sub, :]
+        for o in range(1, nz):
+            gp_copy(o).wait_send()
+
+        @pl.when(at_top)
+        def _():
+            go(1)
+
         for o in range(1, nd):
             gn_copy(o).start()
         gnr_buf[d] = gns_buf[d]
+        for o in range(1, plane):
+            dt_copy(o).wait_recv()
+        for zt in range(nz):
+            dots = dot_buf[zt]
+            for dt in range(1, nd):
+                dots = dots + dot_buf[dt * nz + zt]
+            turn_buf[...] = jnp.broadcast_to(dots[:1, :] * (1.0 / width), (tok, tok)).T
+            mean_buf[zt] = turn_buf[pl.ds(sub_start_d, sub), :]
         for o in range(1, nd):
             gn_copy(o).wait_recv()
         grad_norm = gnr_buf[0].astype(F32)
@@ -230,24 +300,13 @@
             grad_norm = grad_norm + gnr_buf[dt].astype(F32)
         grad_norm = grad_norm.astype(BF16).astype(F32).reshape(tok, feat)
         scaled = grad_norm * gain_ref[:, pl.ds(z_start, feat)]
-        x_z = x_ref[:, pl.ds(z_start, feat)].astype(F32)
-        x_all = x_ref[...].astype(F32)
-        rad = jnp.sqrt(jnp.mean(x_all * x_all, axis=1, keepdims=True) + eps)
-        normed = x_z / rad
-        own_dot = jnp.sum(scaled * normed, axis=1, keepdims=True)
-        dot_buf[z] = jnp.broadcast_to(own_dot, (tok, tok)).T[:8, :]
-        for o in range(1, nz):
-            dt_copy(o).start()
+        normed = norm_buf[...]
+        rad = rad_buf[:, :1]
+        mean_dot = mean_buf[...].reshape(tok, tok)[:, :1]
         if sections > 2:
             @pl.when(jnp.logical_not(at_top))
             def _():
                 uii_copy().wait_recv()
-        for o in range(1, nz):
-            dt_copy(o).wait_recv()
-        dots = dot_buf[0]
-        for zt in range(1, nz):
-            dots = dots + dot_buf[zt]
-        mean_dot = jnp.broadcast_to(dots[:1, :], (tok, tok)).T[:, :1] * (1.0 / width)
         up_buf[...] = (uii_buf[...].astype(F32) + (scaled - normed * mean_dot) / rad).astype(BF16)
         for zt in range(nz):
             up_copy(zt, d).start()
@@ -285,7 +344,6 @@
         sc_copy(o).start()
 
     for o in range(1, nd):
-        a_copy(o).wait_send()
         inf_copy(o).wait_send()
     for o in range(1, nz):
         p_copy(o).wait_send()
@@ -297,8 +355,7 @@
 
     @pl.when(lower)
     def _():
-        for o in range(1, nz):
-            gp_copy(o).wait_send()
+        for o in range(1, plane):
             dt_copy(o).wait_send()
         for o in range(1, nd):
             gn_copy(o).wait_send()
@@ -335,9 +392,10 @@
     column = sections * nz
     plane = nd * nz
     vmem = pl.BlockSpec(memory_space=pltpu.VMEM)
+    hbm = pl.BlockSpec(memory_space=pl.ANY)
     dma = pltpu.SemaphoreType.DMA
     sems = []
-    for count in (nd, nd, nz, nd, nz, nd, nz):
+    for count in (nd, nd, nz, nd, nz, nd, plane):
         sems += [dma((count,)), dma((count,))]
     sems += [dma((nz,)), dma((nd,)), dma((1,)), dma((1,))]
     sems += [dma((plane,)), dma((plane,)), dma((column,)), dma((column,))]
@@ -347,7 +405,7 @@
             jax.ShapeDtypeStruct((SEQS, piece), F32),
             jax.ShapeDtypeStruct((SEQS, queries), F32),
         ),
-        in_specs=[vmem, vmem, vmem, pl.BlockSpec(memory_space=pltpu.SMEM), vmem, vmem],
+        in_specs=[hbm, hbm, vmem, pl.BlockSpec(memory_space=pltpu.SMEM), hbm, vmem],
         out_specs=(vmem, vmem),
         scratch_shapes=[
             pltpu.VMEM((nd, tok, feat), BF16),
@@ -360,12 +418,21 @@
             pltpu.VMEM((nz, nd, sub, cols), BF16),
             pltpu.VMEM((nd, nz, sub, feat), BF16),
             pltpu.VMEM((nd, nz, sub, feat), BF16),
-            pltpu.VMEM((nz, 8, tok), F32),
+            pltpu.VMEM((plane, 8, tok), F32),
             pltpu.VMEM((tok, feat), BF16),
             pltpu.VMEM((nz, SEQS, piece), F32),
             pltpu.VMEM((plane, SEQS, piece), F32),
             pltpu.VMEM((column, SEQS, queries), F32),
+            pltpu.VMEM((tok, width), BF16),
+            pltpu.VMEM((feat, cols), BF16),
+            pltpu.VMEM((nd, sub, cols), F32),
+            pltpu.VMEM((tok, feat), F32),
+            pltpu.VMEM((tok, 128), F32),
+            pltpu.VMEM((tok, tok), F32),
+            pltpu.VMEM((nz, sub, tok), F32),
             *sems,
+            dma((4,)),
+            pltpu.SemaphoreType.REGULAR((2,)),
         ],
         compiler_params=pltpu.CompilerParams(
             collective_id=0, has_side_effects=True, vmem_limit_bytes=60 * 1024 * 1024

time: 91.1 us -> 74.4 us (0.82)
  Pallas kernels: 87.7 us -> 71 us
    pallas_call x1, Pallas kernels: 87.7 us -> 71 us  [body(): pl.pallas_call(functools.partial(kernel, sections, nd, nz), out_shape=(ja...]
where the time goes in v2:
time: 74.4 us; the launch traced here: 74.1 us
  Pallas kernels  71 us (95%)
  local copies, waits for them, and re-layouts  2.51 us (3%)
    pallas_call x1, Pallas kernels, body(): pl.pallas_call(functools.partial(kernel, sections, nd, nz), out_shape=(ja...  71 us
    unnamed x2, local copies, waits for them, and re-layouts  2.51 us

profile of v2, /device:TPU:0, one launch (start us, length us, event | category | flops | bytes accessed | tf_op | source)
XLA Modules:
  0.0 74.1 jit_solution(7880386345795768336)
XLA Ops:
  0.6 71.0 %shard_map.77 = (f32[2,1024]{1,0:T(2,128)}, f32[2,64]{1,0:T(2,128)}) custom-call(bf16[128,4096]{1,0:T(8,128)(2,1)} %bitcast.5, bf16[1024,1024]{1,0:T(8,128)(2,1)} %bitcast.4, f32[1,4096]{1,0:T(1,128)} %gain_ref.1, s32[1,2]{1,0:T(1,128)} %seed_ref.1, bf16[128,4096]{1,0:T(8,128)(2,1)} %og_ref.1, bf16[64,1024]{1,0:T(8,128)(2,1)} %bitcast.6), custom_call_target="tpu_custom_call" | custom-call | tf_op jit(solution)/shard_map/pallas_call | solution.py:402
  71.6 1.3 %copy.10 = f32[1,2,1024]{2,1,0:T(2,128)} copy(f32[1,2,1024]{2,1,0:T(2,128)} %bitcast.7) | data formatting | bytes 16384
  72.9 1.2 %copy.11 = f32[2,64]{1,0:T(2,128)} copy(f32[2,64]{1,0:T(2,128)} %get-tuple-element.9) | data formatting | bytes 1024

commit v3 on v2

--- a/solution.py
+++ b/solution.py
@@ -139,6 +139,14 @@
             a_copy(o).start()
 
     w_load.wait()
+
+    def p_copy(o, block):
+        to = lax.rem(z + o, nz)
+        return remote(
+            ps_buf.at[to, block], pr_buf.at[z, block], p_ss.at[o, block], p_rs.at[o, block],
+            dev(s, d, to),
+        )
+
     for o in range(nd):
         block = lax.rem(d + nd - o, nd)
         if o:
@@ -147,6 +155,11 @@
         for zt in range(nz):
             ps_buf[zt, block] = part[zt * sub : (zt + 1) * sub, :]
 
+        @pl.when(jnp.logical_not(below_top))
+        def _():
+            for oz in range(1, nz):
+                p_copy(oz, block).start()
+
     for o in range(1, nd):
         a_copy(o).wait_send()
 
@@ -163,23 +176,41 @@
         @pl.when(below_top)
         def _():
             pl.semaphore_wait(go_sem.at[1], 1)
-
-    def p_copy(o):
+            for o in range(nd):
+                block = lax.rem(d + nd - o, nd)
+                for oz in range(1, nz):
+                    p_copy(oz, block).start()
+
+    table_out = sign_rows(seed_ref[0, 1], d_start, cols, scale)
+
+    def gp_copy(o, block):
         to = lax.rem(z + o, nz)
-        return remote(ps_buf.at[to], pr_buf.at[z], p_ss.at[o], p_rs.at[o], dev(s, d, to))
-
-    for o in range(1, nz):
-        p_copy(o).start()
-    pr_buf[z] = ps_buf[z]
-    table_out = sign_rows(seed_ref[0, 1], d_start, cols, scale)
-    for o in range(1, nz):
-        p_copy(o).wait_recv()
-    summed = pr_buf[0].astype(F32)
-    for zt in range(1, nz):
-        summed = summed + pr_buf[zt].astype(F32)
-    sig = jax.nn.sigmoid(summed)
-    sum_buf[...] = summed
-    slope_buf[...] = sig * (1.0 + summed * (1.0 - sig))
+        return remote(
+            gp_buf.at[z, block], gp_buf.at[z, block], gp_ss.at[o, block], gp_rs.at[o, block],
+            dev(s, d, to),
+        )
+
+    for o in range(nd):
+        block = lax.rem(d + nd - o, nd)
+        summed = ps_buf[z, block].astype(F32)
+        for oz in range(1, nz):
+            p_copy(oz, block).wait_recv()
+            summed = summed + pr_buf[lax.rem(z + nz - oz, nz), block].astype(F32)
+        sig = jax.nn.sigmoid(summed)
+        slope = sig * (1.0 + summed * (1.0 - sig))
+        sum_buf[block] = summed
+        slope_buf[block] = slope
+
+        @pl.when(at_top)
+        def _():
+            if o:
+                og_copy(o).wait_recv()
+            else:
+                ui_load().wait()
+            gp_buf[z, block] = (ui_buf[block].astype(F32) * slope).astype(BF16)
+            if sections > 1:
+                for oz in range(1, nz):
+                    gp_copy(oz, block).start()
 
     def up_copy(zt, source):
         return remote(
@@ -192,23 +223,21 @@
 
     @pl.when(at_top)
     def _():
-        for o in range(1, nd):
-            og_copy(o).wait_recv()
-        ui_load().wait()
         uii_load().wait()
 
     @pl.when(jnp.logical_not(at_top))
     def _():
         for source in range(nd):
             up_copy(0, source).wait_recv()
-
-    grad_pre = (ui_buf[...].astype(F32) * slope_buf[...]).astype(BF16)
-    gp_buf[z] = grad_pre
-
-    def gp_copy(o):
-        to = lax.rem(z + o, nz)
-        return remote(gp_buf.at[z], gp_buf.at[z], gp_ss.at[o], gp_rs.at[o], dev(s, d, to))
-
+        gp_buf[z] = (ui_buf[...].astype(F32) * slope_buf[...]).astype(BF16)
+
+        @pl.when(lower)
+        def _():
+            for block in range(nd):
+                for oz in range(1, nz):
+                    gp_copy(oz, block).start()
+
+    grad_pre = gp_buf[z]
     plane = nd * nz
     mine = d * nz + z
 
@@ -221,8 +250,6 @@
 
     @pl.when(lower)
     def _():
-        for o in range(1, nz):
-            gp_copy(o).start()
         pre = gp_buf[z].astype(F32) * sum_buf[...]
         own_dot = jnp.sum(pre.reshape(nd * sub, cols), axis=1, keepdims=True)
         dot_buf[mine] = jnp.broadcast_to(own_dot, (tok, tok)).T[:8, :]
@@ -262,29 +289,30 @@
     gr_buf[mine] = g_buf[z]
 
     def gn_copy(o):
-        to = lax.rem(d + o, nd)
+        to = lax.rem(d + nd - o, nd)
         return remote(gns_buf.at[to], gnr_buf.at[d], gn_ss.at[o], gn_rs.at[o], dev(s, to, z))
 
     @pl.when(lower)
     def _():
-        for o in range(nz):
-            block = lax.rem(z + nz - o, nz)
+        for o in range(nd):
+            block = lax.rem(d + nd - o, nd)
+            for oz in range(1, nz):
+                gp_copy(oz, block).wait_recv()
+            rows = gp_buf[:, block].reshape(tok, cols)
+            part = lax.dot_general(rows, w_ref[...], NT, preferred_element_type=F32).astype(BF16)
             if o:
-                gp_copy(o).wait_recv()
-            rows = gp_buf[block].reshape(nd * sub, cols)
-            part = lax.dot_general(rows, w_ref[...], NT, preferred_element_type=F32).astype(BF16)
-            for dt in range(nd):
-                gns_buf[dt, block] = part[dt * sub : (dt + 1) * sub, :]
-        for o in range(1, nz):
-            gp_copy(o).wait_send()
+                gns_buf[block] = part
+                gn_copy(o).start()
+            else:
+                gnr_buf[d] = part
+        for block in range(nd):
+            for oz in range(1, nz):
+                gp_copy(oz, block).wait_send()
 
         @pl.when(at_top)
         def _():
             go(1)
 
-        for o in range(1, nd):
-            gn_copy(o).start()
-        gnr_buf[d] = gns_buf[d]
         for o in range(1, plane):
             dt_copy(o).wait_recv()
         for zt in range(nz):
@@ -298,7 +326,7 @@
         grad_norm = gnr_buf[0].astype(F32)
         for dt in range(1, nd):
             grad_norm = grad_norm + gnr_buf[dt].astype(F32)
-        grad_norm = grad_norm.astype(BF16).astype(F32).reshape(tok, feat)
+        grad_norm = grad_norm.astype(BF16).astype(F32)
         scaled = grad_norm * gain_ref[:, pl.ds(z_start, feat)]
         normed = norm_buf[...]
         rad = rad_buf[:, :1]
@@ -345,8 +373,9 @@
 
     for o in range(1, nd):
         inf_copy(o).wait_send()
-    for o in range(1, nz):
-        p_copy(o).wait_send()
+    for block in range(nd):
+        for oz in range(1, nz):
+            p_copy(oz, block).wait_send()
 
     @pl.when(at_top)
     def _():
@@ -395,8 +424,8 @@
     hbm = pl.BlockSpec(memory_space=pl.ANY)
     dma = pltpu.SemaphoreType.DMA
     sems = []
-    for count in (nd, nd, nz, nd, nz, nd, plane):
-        sems += [dma((count,)), dma((count,))]
+    for shape in ((nd,), (nd,), (nz, nd), (nd,), (nz, nd), (nd,), (plane,)):
+        sems += [dma(shape), dma(shape)]
     sems += [dma((nz,)), dma((nd,)), dma((1,)), dma((1,))]
     sems += [dma((plane,)), dma((plane,)), dma((column,)), dma((column,))]
     grads, scores = pl.pallas_call(
@@ -416,8 +445,8 @@
             pltpu.VMEM((nd, sub, cols), BF16),
             pltpu.VMEM((tok, feat), BF16),
             pltpu.VMEM((nz, nd, sub, cols), BF16),
-            pltpu.VMEM((nd, nz, sub, feat), BF16),
-            pltpu.VMEM((nd, nz, sub, feat), BF16),
+            pltpu.VMEM((nd, tok, feat), BF16),
+            pltpu.VMEM((nd, tok, feat), BF16),
             pltpu.VMEM((plane, 8, tok), F32),
             pltpu.VMEM((tok, feat), BF16),
             pltpu.VMEM((nz, SEQS, piece), F32),

time: 74.4 us -> 67.7 us (0.910)
  Pallas kernels: 71 us -> 64.2 us
    pallas_call x1, Pallas kernels: 71 us -> 64.2 us  [body(): pl.pallas_call(functools.partial(kernel, sections, nd, nz), out_shape=(ja...]
where the time goes in v3:
time: 67.7 us; the launch traced here: 67.4 us
  Pallas kernels  64.2 us (95%)
  local copies, waits for them, and re-layouts  2.51 us (4%)
    pallas_call x1, Pallas kernels, body(): pl.pallas_call(functools.partial(kernel, sections, nd, nz), out_shape=(ja...  64.2 us
    unnamed x2, local copies, waits for them, and re-layouts  2.51 us

profile of v3, /device:TPU:0, one launch (start us, length us, event | category | flops | bytes accessed | tf_op | source)
XLA Modules:
  0.0 67.4 jit_solution(12420463625749544704)
XLA Ops:
  0.6 64.2 %shard_map.77 = (f32[2,1024]{1,0:T(2,128)}, f32[2,64]{1,0:T(2,128)}) custom-call(bf16[128,4096]{1,0:T(8,128)(2,1)} %bitcast.5, bf16[1024,1024]{1,0:T(8,128)(2,1)} %bitcast.4, f32[1,4096]{1,0:T(1,128)} %gain_ref.1, s32[1,2]{1,0:T(1,128)} %seed_ref.1, bf16[128,4096]{1,0:T(8,128)(2,1)} %og_ref.1, bf16[64,1024]{1,0:T(8,128)(2,1)} %bitcast.6), custom_call_target="tpu_custom_call" | custom-call | tf_op jit(solution)/shard_map/pallas_call | solution.py:431
  64.9 1.3 %copy.10 = f32[1,2,1024]{2,1,0:T(2,128)} copy(f32[1,2,1024]{2,1,0:T(2,128)} %bitcast.7) | data formatting | bytes 16384
  66.2 1.2 %copy.11 = f32[2,64]{1,0:T(2,128)} copy(f32[2,64]{1,0:T(2,128)} %get-tuple-element.9) | data formatting | bytes 1024

commit v4 on v3

--- a/solution.py
+++ b/solution.py
@@ -31,10 +31,10 @@
 def kernel(
     sections, nd, nz,
     x_hbm, w_hbm, gain_ref, seed_ref, og_ref, q_ref,
-    grads_ref, scores_ref,
+    out_ref,
     a_buf, inf_buf, ps_buf, pr_buf, slope_buf, ui_buf, uii_buf, gp_buf,
     gns_buf, gnr_buf, dot_buf, up_buf, g_buf, gr_buf, sc_buf,
-    x_ref, w_ref, sum_buf, norm_buf, rad_buf, turn_buf, mean_buf,
+    x_ref, w_ref, sum_buf, norm_buf, rad_buf, turn_buf, mean_buf, left_buf, pick_buf,
     a_ss, a_rs, inf_ss, inf_rs, p_ss, p_rs, og_ss, og_rs, gp_ss, gp_rs,
     gn_ss, gn_rs, dt_ss, dt_rs, up_ss, up_rs, uii_ss, uii_rs,
     g_ss, g_rs, sc_ss, sc_rs, in_sem, go_sem,
@@ -118,20 +118,6 @@
         ui_load().start()
         uii_load().start()
 
-    scale = 1.0 / math.sqrt(width)
-    x_sub = x_ref[pl.ds(sub_start, sub), :].astype(F32)
-    radius_sub = jnp.sqrt(jnp.mean(x_sub * x_sub, axis=1, keepdims=True) + eps)
-    lifted_sub = (x_sub / radius_sub * gain_ref[...]).astype(BF16)
-    table_in = sign_rows(seed_ref[0, 0], 0, width, scale)
-    inf_buf[d] = lax.dot_general(lifted_sub, table_in, NT, preferred_element_type=F32)
-
-    def inf_copy(o):
-        to = lax.rem(d + o, nd)
-        return remote(inf_buf.at[d], inf_buf.at[d], inf_ss.at[o], inf_rs.at[o], dev(s, to, z))
-
-    for o in range(1, nd):
-        inf_copy(o).start()
-
     @pl.when(below_top)
     def _():
         pl.semaphore_wait(go_sem.at[0], 1)
@@ -173,6 +159,40 @@
         def _():
             go(0)
 
+    scale = 1.0 / math.sqrt(width)
+    x_sub = x_ref[pl.ds(sub_start, sub), :].astype(F32)
+    radius_sub = jnp.sqrt(jnp.mean(x_sub * x_sub, axis=1, keepdims=True) + eps)
+    lifted_sub = (x_sub / radius_sub * gain_ref[...]).astype(BF16)
+    table_in = sign_rows(seed_ref[0, 0], 0, width, scale)
+    inf_buf[d] = lax.dot_general(lifted_sub, table_in, NT, preferred_element_type=F32)
+
+    def inf_copy(o):
+        to = lax.rem(d + o, nd)
+        return remote(inf_buf.at[d], inf_buf.at[d], inf_ss.at[o], inf_rs.at[o], dev(s, to, z))
+
+    for o in range(1, nd):
+        inf_copy(o).start()
+
+
+    piece = R * R // nz
+    per_seq = nd * sub // SEQS
+
+    def spread():
+        for o in range(1, nd):
+            inf_copy(o).wait_recv()
+        in_feat = inf_buf[...].reshape(nd * sub, R).astype(BF16)
+        for zt in range(nz):
+            entry = lax.broadcasted_iota(jnp.int32, (R, piece), 1) + zt * piece
+            which = lax.broadcasted_iota(jnp.int32, (R, piece), 0)
+            pick_in = (entry // R == which).astype(F32).astype(BF16)
+            pick_buf[zt] = (entry % R == which).astype(F32).astype(BF16)
+            left_buf[zt] = jnp.dot(in_feat, pick_in, preferred_element_type=F32)
+
+    @pl.when(jnp.logical_not(at_top))
+    def _():
+        spread()
+
+    if sections > 1:
         @pl.when(below_top)
         def _():
             pl.semaphore_wait(go_sem.at[1], 1)
@@ -224,6 +244,7 @@
     @pl.when(at_top)
     def _():
         uii_load().wait()
+        spread()
 
     @pl.when(jnp.logical_not(at_top))
     def _():
@@ -256,22 +277,11 @@
         for o in range(1, plane):
             dt_copy(o).start()
 
-    for o in range(1, nd):
-        inf_copy(o).wait_recv()
     out_feat = lax.dot_general(
         grad_pre.reshape(nd * sub, cols), table_out, NT, preferred_element_type=F32
     ).astype(BF16)
-    in_feat = inf_buf[...].reshape(nd * sub, R).astype(BF16)
-    piece = R * R // nz
-    per_seq = nd * sub // SEQS
     for zt in range(nz):
-        entry = lax.broadcasted_iota(jnp.int32, (R, piece), 1) + zt * piece
-        which = lax.broadcasted_iota(jnp.int32, (R, piece), 0)
-        pick_in = (entry // R == which).astype(F32).astype(BF16)
-        pick_out = (entry % R == which).astype(F32).astype(BF16)
-        left = jnp.dot(in_feat, pick_in, preferred_element_type=F32)
-        right = jnp.dot(out_feat, pick_out, preferred_element_type=F32)
-        product = left * right
+        product = left_buf[zt] * jnp.dot(out_feat, pick_buf[zt], preferred_element_type=F32)
         for k in range(SEQS):
             g_buf[zt, k : k + 1, :] = jnp.sum(
                 product[k * per_seq : (k + 1) * per_seq], axis=0, keepdims=True
@@ -298,6 +308,15 @@
             block = lax.rem(d + nd - o, nd)
             for oz in range(1, nz):
                 gp_copy(oz, block).wait_recv()
+            if o == nd - 1:
+                for each in range(nd):
+                    for oz in range(1, nz):
+                        gp_copy(oz, each).wait_send()
+
+                @pl.when(at_top)
+                def _():
+                    go(1)
+
             rows = gp_buf[:, block].reshape(tok, cols)
             part = lax.dot_general(rows, w_ref[...], NT, preferred_element_type=F32).astype(BF16)
             if o:
@@ -305,14 +324,6 @@
                 gn_copy(o).start()
             else:
                 gnr_buf[d] = part
-        for block in range(nd):
-            for oz in range(1, nz):
-                gp_copy(oz, block).wait_send()
-
-        @pl.when(at_top)
-        def _():
-            go(1)
-
         for o in range(1, plane):
             dt_copy(o).wait_recv()
         for zt in range(nz):
@@ -348,7 +359,7 @@
     grads = gr_buf[0]
     for other in range(1, plane):
         grads = grads + gr_buf[other]
-    grads_ref[...] = grads
+    out_ref[:, :piece] = grads
     queries = q_ref[...]
     high = grads.astype(BF16)
     rest = grads - high.astype(F32)
@@ -402,7 +413,7 @@
     scores = sc_buf[0]
     for other in range(1, column):
         scores = scores + sc_buf[other]
-    scores_ref[...] = scores
+    out_ref[:, piece : piece + scores.shape[1]] = scores
     for o in range(1, column):
         sc_copy(o).wait_send()
 
@@ -428,14 +439,11 @@
         sems += [dma(shape), dma(shape)]
     sems += [dma((nz,)), dma((nd,)), dma((1,)), dma((1,))]
     sems += [dma((plane,)), dma((plane,)), dma((column,)), dma((column,))]
-    grads, scores = pl.pallas_call(
+    out = pl.pallas_call(
         functools.partial(kernel, sections, nd, nz),
-        out_shape=(
-            jax.ShapeDtypeStruct((SEQS, piece), F32),
-            jax.ShapeDtypeStruct((SEQS, queries), F32),
-        ),
+        out_shape=jax.ShapeDtypeStruct((SEQS, piece + queries), F32),
         in_specs=[hbm, hbm, vmem, pl.BlockSpec(memory_space=pltpu.SMEM), hbm, vmem],
-        out_specs=(vmem, vmem),
+        out_specs=vmem,
         scratch_shapes=[
             pltpu.VMEM((nd, tok, feat), BF16),
             pltpu.VMEM((nd, sub, R), F32),
@@ -459,6 +467,8 @@
             pltpu.VMEM((tok, 128), F32),
             pltpu.VMEM((tok, tok), F32),
             pltpu.VMEM((nz, sub, tok), F32),
+            pltpu.VMEM((nz, tok, piece), F32),
+            pltpu.VMEM((nz, R, piece), BF16),
             *sems,
             dma((4,)),
             pltpu.SemaphoreType.REGULAR((2,)),
@@ -467,7 +477,7 @@
             collective_id=0, has_side_effects=True, vmem_limit_bytes=60 * 1024 * 1024
         ),
     )(section_input[0], weights[0], gains, proj_seeds, out_grad, query_grads[0])
-    return (grads[None], scores)
+    return (out[None, :, :piece], out[:, piece:])
 
 
 def solution(mesh):

time: 67.7 us -> 66.4 us (0.981)
  Pallas kernels: 64.2 us -> 62.9 us
    unnamed x2 -> x0, local copies, waits for them, and re-layouts: 2.51 us -> none
    pallas_call x1, Pallas kernels: 64.2 us -> 62.9 us  [body(): pl.pallas_call(functools.partial(kernel, sections, nd, nz), out_shape=jax...]
    broadcast_in_dim x0 -> x1, local copies, waits for them, and re-layouts: none -> 1.29 us  [body(): return (out[None, :, :piece], out[:, piece:])]
    slice x0 -> x1, local copies, waits for them, and re-layouts: none -> 1.23 us  [body(): return (out[None, :, :piece], out[:, piece:])]
where the time goes in v4:
time: 66.4 us; the launch traced here: 66 us
  Pallas kernels  62.9 us (95%)
  local copies, waits for them, and re-layouts  2.52 us (4%)
    pallas_call x1, Pallas kernels, body(): pl.pallas_call(functools.partial(kernel, sections, nd, nz), out_shape=jax...  62.9 us

profile of v4, /device:TPU:0, one launch (start us, length us, event | category | flops | bytes accessed | tf_op | source)
XLA Modules:
  0.0 66.0 jit_solution(1967000075148981870)
XLA Ops:
  0.6 62.9 %shard_map.77 = f32[2,1088]{1,0:T(2,128)} custom-call(bf16[128,4096]{1,0:T(8,128)(2,1)} %bitcast.6, bf16[1024,1024]{1,0:T(8,128)(2,1)} %bitcast.5, f32[1,4096]{1,0:T(1,128)} %gain_ref.1, s32[1,2]{1,0:T(1,128)} %seed_ref.1, bf16[128,4096]{1,0:T(8,128)(2,1)} %og_ref.1, bf16[64,1024]{1,0:T(8,128)(2,1)} %bitcast.7), custom_call_target="tpu_custom_call" | custom-call | tf_op jit(solution)/shard_map/pallas_call | solution.py:442
  63.5 1.2 %slice.7 = f32[2,64]{1,0:T(2,128)} slice(f32[2,1088]{1,0:T(2,128)} %shard_map.77), slice={[0:2], [1024:1088]} | slice | bytes 1024 | tf_op jit(solution)/shard_map/slice | solution.py:480
  64.7 1.3 %slice_bitcast_fusion = f32[1,2,1024]{2,1,0:T(2,128)} fusion(f32[2,1088]{1,0:T(2,128)} %shard_map.77), kind=kLoop, calls=%fused_computation | loop fusion | bytes 16384 | tf_op jit(solution)/shard_map/broadcast_in_dim | solution.py:480

commit v5 on v4

--- a/solution.py
+++ b/solution.py
@@ -37,7 +37,7 @@
     x_ref, w_ref, sum_buf, norm_buf, rad_buf, turn_buf, mean_buf, left_buf, pick_buf,
     a_ss, a_rs, inf_ss, inf_rs, p_ss, p_rs, og_ss, og_rs, gp_ss, gp_rs,
     gn_ss, gn_rs, dt_ss, dt_rs, up_ss, up_rs, uii_ss, uii_rs,
-    g_ss, g_rs, sc_ss, sc_rs, in_sem, go_sem,
+    g_ss, g_rs, sc_ss, sc_rs, in_sem, go_sem, far_sem,
 ):
     s = lax.axis_index("section")
     d = lax.axis_index("dp")
@@ -68,16 +68,21 @@
     w_load.start()
 
     barrier = pltpu.get_barrier_semaphore()
-    total = sections * nd * nz
-    me = (s * nd + d) * nz + z
-
-    @pl.loop(1, total)
-    def _(step):
-        other = lax.rem(me + step, total)
+    column = sections * nz
+    here = s * nz + z
+
+    def signal_column(sem):
+        for o in range(1, column):
+            to = lax.rem(here + o, column)
+            pl.semaphore_signal(
+                sem, inc=1, device_id=dev(to // nz, d, lax.rem(to, nz)), device_id_type=MESH
+            )
+
+    for o in range(1, nd):
         pl.semaphore_signal(
-            barrier, inc=1, device_id_type=MESH,
-            device_id=dev(other // (nd * nz), lax.rem(other // nz, nd), lax.rem(other, nz)),
-        )
+            barrier, inc=1, device_id=dev(s, lax.rem(d + o, nd), z), device_id_type=MESH
+        )
+    signal_column(barrier)
 
     x_load.wait()
     hidden = x_ref[...].astype(F32)
@@ -88,7 +93,7 @@
     rad_buf[...] = jnp.broadcast_to(radius, rad_buf.shape)
     a_buf[d] = (normed_z * gain_z).astype(BF16)
 
-    pl.semaphore_wait(barrier, total - 1)
+    pl.semaphore_wait(barrier, nd - 1 + column - 1)
 
     def a_copy(o):
         to = lax.rem(d + o, nd)
@@ -123,6 +128,8 @@
         pl.semaphore_wait(go_sem.at[0], 1)
         for o in range(1, nd):
             a_copy(o).start()
+
+    signal_column(far_sem.at[0])
 
     w_load.wait()
 
@@ -258,6 +265,7 @@
                 for oz in range(1, nz):
                     gp_copy(oz, block).start()
 
+    pl.semaphore_wait(far_sem.at[0], column - 1)
     grad_pre = gp_buf[z]
     plane = nd * nz
     mine = d * nz + z
@@ -368,8 +376,6 @@
     part = lax.dot_general(high, queries, NT, preferred_element_type=F32)
     part = part + lax.dot_general(middle, queries, NT, preferred_element_type=F32)
     part = part + lax.dot_general(low, queries, NT, preferred_element_type=F32)
-    column = sections * nz
-    here = s * nz + z
     sc_buf[here] = part
 
     def sc_copy(o):
@@ -472,6 +478,7 @@
             *sems,
             dma((4,)),
             pltpu.SemaphoreType.REGULAR((2,)),
+            pltpu.SemaphoreType.REGULAR((1,)),
         ],
         compiler_params=pltpu.CompilerParams(
             collective_id=0, has_side_effects=True, vmem_limit_bytes=60 * 1024 * 1024

time: 66.4 us -> 65.3 us (0.983)
  Pallas kernels: 62.9 us -> 61.8 us
    pallas_call x1, Pallas kernels: 62.9 us -> 61.8 us  [body(): pl.pallas_call(functools.partial(kernel, sections, nd, nz), out_shape=jax...]
where the time goes in v5:
time: 65.3 us; the launch traced here: 65 us
  Pallas kernels  61.8 us (95%)
  local copies, waits for them, and re-layouts  2.52 us (4%)
    pallas_call x1, Pallas kernels, body(): pl.pallas_call(functools.partial(kernel, sections, nd, nz), out_shape=jax...  61.8 us

profile of v5, /device:TPU:0, one launch (start us, length us, event | category | flops | bytes accessed | tf_op | source)
XLA Modules:
  0.0 65.0 jit_solution(2992173582641001330)
XLA Ops:
  0.6 61.8 %shard_map.77 = f32[2,1088]{1,0:T(2,128)} custom-call(bf16[128,4096]{1,0:T(8,128)(2,1)} %bitcast.6, bf16[1024,1024]{1,0:T(8,128)(2,1)} %bitcast.5, f32[1,4096]{1,0:T(1,128)} %gain_ref.1, s32[1,2]{1,0:T(1,128)} %seed_ref.1, bf16[128,4096]{1,0:T(8,128)(2,1)} %og_ref.1, bf16[64,1024]{1,0:T(8,128)(2,1)} %bitcast.7), custom_call_target="tpu_custom_call" | custom-call | tf_op jit(solution)/shard_map/pallas_call | solution.py:448
  62.5 1.2 %slice.7 = f32[2,64]{1,0:T(2,128)} slice(f32[2,1088]{1,0:T(2,128)} %shard_map.77), slice={[0:2], [1024:1088]} | slice | bytes 1024 | tf_op jit(solution)/shard_map/slice | solution.py:487
  63.7 1.3 %slice_bitcast_fusion = f32[1,2,1024]{2,1,0:T(2,128)} fusion(f32[2,1088]{1,0:T(2,128)} %shard_map.77), kind=kLoop, calls=%fused_computation | loop fusion | bytes 16384 | tf_op jit(solution)/shard_map/broadcast_in_dim | solution.py:487

commit v6 on v5

--- a/solution.py
+++ b/solution.py
@@ -342,20 +342,18 @@
             mean_buf[zt] = turn_buf[pl.ds(sub_start_d, sub), :]
         for o in range(1, nd):
             gn_copy(o).wait_recv()
-        grad_norm = gnr_buf[0].astype(F32)
-        for dt in range(1, nd):
-            grad_norm = grad_norm + gnr_buf[dt].astype(F32)
-        grad_norm = grad_norm.astype(BF16).astype(F32)
-        scaled = grad_norm * gain_ref[:, pl.ds(z_start, feat)]
-        normed = norm_buf[...]
-        rad = rad_buf[:, :1]
-        mean_dot = mean_buf[...].reshape(tok, tok)[:, :1]
         if sections > 2:
             @pl.when(jnp.logical_not(at_top))
             def _():
                 uii_copy().wait_recv()
-        up_buf[...] = (uii_buf[...].astype(F32) + (scaled - normed * mean_dot) / rad).astype(BF16)
         for zt in range(nz):
+            rows = pl.ds(zt * sub, sub)
+            grad_norm = gnr_buf[0, rows].astype(F32)
+            for dt in range(1, nd):
+                grad_norm = grad_norm + gnr_buf[dt, rows].astype(F32)
+            scaled = grad_norm.astype(BF16).astype(F32) * gain_ref[:, pl.ds(z_start, feat)]
+            change = (scaled - norm_buf[rows] * mean_buf[zt][:, :1]) / rad_buf[rows, :1]
+            up_buf[rows] = (uii_buf[rows].astype(F32) + change).astype(BF16)
             up_copy(zt, d).start()
         if sections > 2:
             @pl.when(s > 1)
@@ -422,6 +420,12 @@
     out_ref[:, piece : piece + scores.shape[1]] = scores
     for o in range(1, column):
         sc_copy(o).wait_send()
+
+
+def part_outputs(both_ref, grads_ref, scores_ref):
+    piece = grads_ref.shape[1]
+    grads_ref[...] = both_ref[:, :piece]
+    scores_ref[...] = both_ref[:, piece : piece + scores_ref.shape[1]]
 
 
 def body(section_input, weights, gains, proj_seeds, out_grad, query_grads):
@@ -484,7 +488,16 @@
             collective_id=0, has_side_effects=True, vmem_limit_bytes=60 * 1024 * 1024
         ),
     )(section_input[0], weights[0], gains, proj_seeds, out_grad, query_grads[0])
-    return (out[None, :, :piece], out[:, piece:])
+    grads, scores = pl.pallas_call(
+        part_outputs,
+        out_shape=(
+            jax.ShapeDtypeStruct((SEQS, piece), F32),
+            jax.ShapeDtypeStruct((SEQS, queries), F32),
+        ),
+        in_specs=[vmem],
+        out_specs=(vmem, vmem),
+    )(out)
+    return (grads[None], scores)
 
 
 def solution(mesh):

time: 65.3 us -> 64.1 us (0.982)
  local copies, waits for them, and re-layouts: 2.52 us -> 0 us
  Pallas kernels: 61.8 us -> 63.1 us
    pallas_call x0 -> x1, Pallas kernels: none -> 1.3 us  [body(): pl.pallas_call(part_outputs, out_shape=(jax.ShapeDtypeStruct((SEQS, piece...]
    broadcast_in_dim x1 -> x0, local copies, waits for them, and re-layouts: 1.29 us -> none  [body(): return (out[None, :, :piece], out[:, piece:])]
    slice x1 -> x0, local copies, waits for them, and re-layouts: 1.23 us -> none  [body(): return (out[None, :, :piece], out[:, piece:])]
where the time goes in v6:
time: 64.1 us; the launch traced here: 63.8 us
  Pallas kernels  63.1 us (98%)
    pallas_call x1, Pallas kernels, body(): pl.pallas_call(functools.partial(kernel, sections, nd, nz), out_shape=jax...  61.8 us
    pallas_call x1, Pallas kernels, body(): pl.pallas_call(part_outputs, out_shape=(jax.ShapeDtypeStruct((SEQS, piece...  1.3 us

profile of v6, /device:TPU:0, one launch (start us, length us, event | category | flops | bytes accessed | tf_op | source)
XLA Modules:
  0.0 63.8 jit_solution(13706133538722792688)
XLA Ops:
  0.6 61.8 %shard_map.77.both_ref = f32[2,1088]{1,0:T(2,128)} custom-call(bf16[128,4096]{1,0:T(8,128)(2,1)} %bitcast.5, bf16[1024,1024]{1,0:T(8,128)(2,1)} %bitcast.4, f32[1,4096]{1,0:T(1,128)} %gain_ref.1, s32[1,2]{1,0:T(1,128)} %seed_ref.1, bf16[128,4096]{1,0:T(8,128)(2,1)} %og_ref.1, bf16[64,1024]{1,0:T(8,128)(2,1)} %bitcast.6), custom_call_target="tpu_custom_call" | custom-call | tf_op jit(solution)/shard_map/pallas_call | solution.py:452
  62.4 1.3 %shard_map.78 = (f32[2,1024]{1,0:T(2,128)}, f32[2,64]{1,0:T(2,128)}) custom-call(f32[2,1088]{1,0:T(2,128)} %shard_map.77.both_ref), custom_call_target="tpu_custom_call" | custom-call | tf_op jit(solution)/shard_map/pallas_call | solution.py:491
